TPU v7x, 32 devices: a whole 2x2x4 slice. The times are simulated.
32 devices in a mesh: member: 8 (over z, y), region: 4 (over x, core).
Axes of the slice: x: 2, y: 2, z: 4, core: 2. Of those that a mesh axis runs over, the one named last changes fastest.
Arguments:
- background_realizations: float32 [1024, 32768], P('member', 'region'), may hold values from -6 to 6
- realization_expected_data: float32 [1024, 16384], P('member', 'region'), may hold values from -6 to 6
- departure_values: float32 [1024, 16384], P('member', 'region'), may hold values from -6 to 6
- instrument_dispersion: float32 [16384], P('region'), may hold values from 0.5 to 2
- window_piece_offsets: int32 [4, 9], P('region'), may hold values from 0 to 64, as said below
- window_data_pieces: int32 [4, 8, 4], P('region'), may hold values from 0 to 39, as said below
- neighbor_piece_ids: int32 [4, 2, 4], P('region'), may hold values from 0 to 31, as said below
- coupling_indicator: int32 [4, 64, 4], P('region'), may hold values 0 or 1
Outputs:
- analysis: float32 [1024, 32768], P('member', 'region')
Inputs may be any that keep to these rules, and one draw needn't show every extreme that they name: `window_piece_offsets`: each row starts at 0, ends at 64 and rises by 1 or more at each entry; entry p lies within 3 of p * 8; in every row one patch spans exactly 14 blocks. `window_data_pieces`: entries index a region's extended observation blocks: 0 to 31 its own, then 4 received from the region before it, then 4 from the region after it; the 4 entries of a patch differ. `neighbor_piece_ids`: entries index the sending region's own observation blocks; the 4 entries of a row differ.
All inputs are finite; a program needn't handle non-finite values. No bound on the sum of `coupling_indicator` on one device may be relied on, other than what follows from the above.
Results may differ from a plain program's by a relative error of at most 0.0003.
Values sent between devices are 32-bit elements; how exact they have to be, the bound alone decides.
A program may use at most 128 MiB of HBM per device.

v0:
```python
import jax
import jax.numpy as jnp
from jax import lax
from jax.sharding import PartitionSpec as P

PIECE_LENGTH = 128
OBS_PER = 4
LOCAL = 512


highest = lax.Precision.HIGHEST


def from_behind(block, axis, distance):
    devices = range(lax.axis_size(axis))
    route = [((i - distance) % len(devices), i) for i in devices]
    return lax.ppermute(block, axis, route)


def from_neighbour(pieces, offset):
    return from_behind((pieces[0], pieces[1], pieces[2]), "region", offset)


def local_solve(expected_data, innovated, variance):
    realization_records = expected_data.shape[0]
    perturbed = expected_data - jnp.mean(expected_data, axis=0, keepdims=True)
    cov_obs = jnp.dot(
        perturbed.T, perturbed, precision=highest, preferred_element_type=jnp.float32
    ) / (realization_records - 1.0)
    cov_obs = cov_obs + jnp.diag(variance)
    factor = jnp.linalg.cholesky(cov_obs)
    weights = jax.scipy.linalg.cho_solve((factor, True), innovated.T)
    return (perturbed, weights)


def update(centred, perturbed, weights, cover_rows):
    realization_records, row_count = centred.shape
    block_rows = row_count // PIECE_LENGTH
    kalman_gain = lax.dot_general(
        centred,
        perturbed,
        (((0,), (0,)), ((), ())),
        precision=highest,
        preferred_element_type=jnp.float32,
    ) / (realization_records - 1.0)
    kalman_gain = (
        kalman_gain.reshape(block_rows, PIECE_LENGTH, OBS_PER, PIECE_LENGTH)
        * cover_rows[:, None, :, None]
    )
    kalman_gain = kalman_gain.reshape(row_count, OBS_PER * PIECE_LENGTH)
    return lax.dot_general(
        weights,
        kalman_gain,
        (((0,), (1,)), ((), ())),
        precision=highest,
        preferred_element_type=jnp.float32,
    )


def body(
    background_realizations,
    realization_expected_data,
    departure_values,
    instrument_dispersion,
    window_piece_offsets,
    window_data_pieces,
    neighbor_piece_ids,
    coupling_indicator,
):
    groups = lax.axis_size("member")
    own_index = lax.axis_index("member")
    neighbor_realization_records, variable_total = background_realizations.shape
    segment_total = variable_total // PIECE_LENGTH
    per_device = segment_total // groups
    spread = (per_device - 1) // 2
    patch_most = per_device + 2 * spread
    gathered_data = realization_expected_data.shape[1] // PIECE_LENGTH
    expected_pieces = realization_expected_data.reshape(
        neighbor_realization_records, gathered_data, PIECE_LENGTH
    )
    innov_blocks = departure_values.reshape(
        neighbor_realization_records, gathered_data, PIECE_LENGTH
    )
    var_blocks = instrument_dispersion.reshape(gathered_data, PIECE_LENGTH)
    halo_rows = neighbor_piece_ids[0]

    def listed(row):
        return (
            jnp.take(expected_pieces, row, axis=1),
            jnp.take(innov_blocks, row, axis=1),
            jnp.take(var_blocks, row, axis=0),
        )

    from_before = from_neighbour(listed(halo_rows[0]), 1)
    from_after = from_neighbour(listed(halo_rows[1]), -1)
    pred_ext = jnp.concatenate([expected_pieces, from_before[0], from_after[0]], axis=1)
    innov_ext = jnp.concatenate([innov_blocks, from_before[1], from_after[1]], axis=1)
    var_ext = jnp.concatenate([var_blocks, from_before[2], from_after[2]], axis=0)
    chosen = window_data_pieces[0]
    flat_list = chosen.reshape(-1)
    send_pred = jnp.take(pred_ext, flat_list, axis=1).reshape(
        neighbor_realization_records, groups * LOCAL
    )
    send_innov = jnp.take(innov_ext, flat_list, axis=1).reshape(
        neighbor_realization_records, groups * LOCAL
    )
    expected_data, innovated = (
        lax.all_to_all(send_pred, "member", split_axis=1, concat_axis=0, tiled=True),
        lax.all_to_all(send_innov, "member", split_axis=1, concat_axis=0, tiled=True),
    )
    own_list = lax.dynamic_index_in_dim(chosen, own_index, 0, keepdims=False)
    variance = jnp.take(var_ext, own_list, axis=0).reshape(LOCAL)
    perturbed, weights = local_solve(expected_data, innovated, variance)
    bounds_row = window_piece_offsets[0]
    starts = bounds_row[:-1]
    cover_all = coupling_indicator[0].astype(jnp.float32)
    lengths = bounds_row[1:] - starts
    slot_ids = jnp.arange(patch_most)
    block_index = jnp.minimum(starts[:, None] + slot_ids[None, :], segment_total - 1)
    in_patch = slot_ids[None, :] < lengths[:, None]
    segment_roster = background_realizations.reshape(
        neighbor_realization_records, segment_total, PIECE_LENGTH
    )
    outgoing = jnp.take(segment_roster, block_index.reshape(-1), axis=1)
    outgoing = jnp.where(in_patch.reshape(1, -1, 1), outgoing, 0.0).reshape(
        neighbor_realization_records, groups * patch_most * PIECE_LENGTH
    )
    states = lax.all_to_all(outgoing, "member", split_axis=1, concat_axis=0, tiled=True)
    centred = states - jnp.mean(states, axis=0, keepdims=True)
    own_slots = lax.dynamic_index_in_dim(block_index, own_index, 0, keepdims=False)
    own_cover = jnp.take(cover_all, own_slots, axis=0)
    result = states + update(centred, perturbed, weights, own_cover)
    returned = lax.all_to_all(result, "member", split_axis=0, concat_axis=1, tiled=True)
    block_ids = jnp.arange(segment_total)
    owners = jnp.sum((bounds_row[None, 1:-1] <= block_ids[:, None]).astype(jnp.int32), axis=1)
    patch_ids = jnp.arange(groups)
    owner_start = jnp.sum(
        jnp.where(owners[:, None] == patch_ids[None, :], starts[None, :], 0), axis=1
    )
    positions = owners * patch_most + block_ids - owner_start
    analysis = jnp.take(
        returned.reshape(neighbor_realization_records, groups * patch_most, PIECE_LENGTH),
        positions,
        axis=1,
    ).reshape(neighbor_realization_records, variable_total)
    return analysis


def solution(mesh):
    return jax.shard_map(
        body,
        mesh=mesh,
        in_specs=(
            P("member", "region"),
            P("member", "region"),
            P("member", "region"),
            P("region"),
            P("region", None),
            P("region", None, None),
            P("region", None, None),
            P("region", None, None),
        ),
        out_specs=P("member", "region"),
        check_vma=False,
    )
```

profile of v0, /device:TPU:0, one launch (start us, length us, event | category | flops | bytes accessed | tf_op | source)
XLA Modules:
  0.0 582.5 jit_solution(13704217409067601463)
XLA Ops:
  4.6 2.9 copy.63
  7.4 1.9 copy.66
  9.4 2.2 gather_fusion.4
  13.4 2.2 gather_fusion.5
  17.1 1.9 collective-permute-start.1
  20.9 3.5 collective-permute-done.1
  24.5 3.3 pad_maximum_fusion
  27.8 3.7 gather_fusion.6
  33.2 3.9 gather_fusion.11
  37.2 4.3 select_bitcast_fusion
  41.4 2.9 copy.60
  44.3 7.5 %all-to-all-start.1 = ((f32[128,8,512]{0,2,1:T(8,128)}), f32[128,8,512]{0,2,1:T(8,128)S(1)}, u32[]{:S(2)}, u32[]{:S(2)}) async-start(f32[128,8,512]{0,2,1:T(8,128)} %bitcast.175), calls=%async_computation.1 | async-start | bytes 4194304 | tf_op jit(solution)/shard_map/all_to_all | solution.py:108
  51.8 2.9 copy.67
  54.7 46.2 %all-to-all-done.1 = f32[128,8,512]{0,2,1:T(8,128)S(1)} async-done(((f32[128,8,512]{0,2,1:T(8,128)}), f32[128,8,512]{0,2,1:T(8,128)S(1)}, u32[]{:S(2)}, u32[]{:S(2)}) %all-to-all-start.1) | async-done | bytes 2097184 | tf_op jit(solution)/shard_map/all_to_all | solution.py:108
  100.9 4.5 all-to-all-start.2
  105.6 5.6 copy.51
  111.2 5.6 copy.52
  116.8 6.2 %gather_fusion = f32[112,128,128]{2,1,0:T(8,128)} fusion(f32[128,64,128]{2,0,1:T(8,128)} %copy.52, s32[1024]{0:T(1024)S(1)} %pad_clamp_fusion.6), kind=kCustom, calls=%fused_computation.8 | custom fusion | bytes 14680512 | tf_op jit(solution)/shard_map/jit(_take)/gather | solution.py:124
  123.0 8.7 %copy.53 = f32[128,112,128]{0,2,1:T(8,128)} copy(f32[128,112,128]{2,0,1:T(8,128)} %bitcast.165) | data formatting | bytes 14680064 | tf_op jit(solution)/shard_map/jit(_take)/gather | solution.py:124
  132.1 7.2 %fusion = f32[128,8,1792]{0,2,1:T(8,128)} fusion(pred[8,1792]{1,0:T(8,128)(4,1)S(1)} %get-tuple-element.50, pred[8,1792]{1,0:T(8,128)(4,1)S(1)} %get-tuple-element.51, f32[128,8,1792]{0,2,1:T(8,128)} %bitcast.164), kind=kLoop, calls=%fused_computation.16 | loop fusion | flops 3670016 | bytes 14708736 | tf_op jit(solution)/shard_map/jit(_where)/select_n | solution.py:125
  139.3 15.6 %all-to-all-done.2 = f32[128,8,512]{0,2,1:T(8,128)} async-done(((f32[128,8,512]{0,2,1:T(8,128)}), f32[128,8,512]{0,2,1:T(8,128)}, u32[]{:S(2)}, u32[]{:S(2)}) %all-to-all-start.2) | async-done | bytes 2097184 | tf_op jit(solution)/shard_map/all_to_all | solution.py:109
  154.9 4.8 all-to-all-start
  161.0 1.9 collective-permute-start.3
  165.1 3.7 fusion.33
  169.4 11.7 %cholesky.103 = f32[128,128]{1,0:T(8,128)S(1)} custom-call(f32[128,128]{1,0:T(8,128)S(1)} %cholesky.263), custom_call_target="Cholesky" | custom-call | tf_op jit(solution)/shard_map/jit(cholesky)/cholesky | solution.py:31
  181.3 9.8 %custom-call.34 = f32[1,128,128]{1,2,0:T(8,128)S(1)} custom-call(f32[1,128,128]{2,1,0:T(8,128)S(1)} %get-tuple-element.39), custom_call_target="InvertDiagBlocksLowerTriangular" | custom-call | tf_op jit(solution)/shard_map/jit(cholesky)/cholesky | solution.py:31
  191.8 12.2 %cholesky.215 = f32[128,128]{1,0:T(8,128)S(1)} custom-call(f32[128,128]{1,0:T(8,128)S(1)} %cholesky.267), custom_call_target="Cholesky" | custom-call | tf_op jit(solution)/shard_map/jit(cholesky)/cholesky | solution.py:31
  203.9 9.8 %custom-call.35 = f32[1,128,128]{1,2,0:T(8,128)S(1)} custom-call(f32[1,128,128]{2,1,0:T(8,128)S(1)} %get-tuple-element.36), custom_call_target="InvertDiagBlocksLowerTriangular" | custom-call | tf_op jit(solution)/shard_map/jit(cholesky)/cholesky | solution.py:31
  214.4 11.7 %cholesky.236 = f32[128,128]{1,0:T(8,128)S(1)} custom-call(f32[128,128]{1,0:T(8,128)S(1)} %cholesky.272), custom_call_target="Cholesky" | custom-call | tf_op jit(solution)/shard_map/jit(cholesky)/cholesky | solution.py:31
  226.2 9.8 %custom-call.36 = f32[1,128,128]{1,2,0:T(8,128)S(1)} custom-call(f32[1,128,128]{2,1,0:T(8,128)S(1)} %get-tuple-element.33), custom_call_target="InvertDiagBlocksLowerTriangular" | custom-call | tf_op jit(solution)/shard_map/jit(cholesky)/cholesky | solution.py:31
  236.6 11.9 %cholesky.253 = f32[128,128]{1,0:T(8,128)S(1)} custom-call(f32[128,128]{1,0:T(8,128)S(1)} %convolution_subtract_fusion.6), custom_call_target="Cholesky" | custom-call | tf_op jit(solution)/shard_map/jit(cholesky)/cholesky | solution.py:31
  253.0 10.0 %while.1 = (s32[]{:T(128)}, f32[512,512]{1,0:T(8,128)S(1)}, s32[4,2]{0,1:T(2,128)S(1)}, f32[4,128,128]{2,1,0:T(8,128)}, s32[]{:T(128)}) while((s32[]{:T(128)}, f32[512,512]{1,0:T(8,128)S(1)}, s32[4,2]{0,1:T(2,128)S(1)}, f32[4,128,128]{2,1,0:T(8,128)}, s32[]{:T(128)}) %tuple.38), condition=%wide.while_cond, body=%wide.while_body.sunk | while | flops 2 | bytes 132705 | solution.py:32
  262.9 40.1 %custom-call.37 = f32[4,128,128]{1,2,0:T(8,128)S(1)} custom-call(f32[4,128,128]{2,1,0:T(8,128)} %get-tuple-element.15), custom_call_target="InvertDiagBlocksLowerTriangular" | custom-call | tf_op jit(solution)/shard_map/jit(_cho_solve)/triangular_solve | solution.py:32
  303.1 2.9 copy.68
  306.0 1.9 copy.69
  318.5 2.1 all-to-all-done
  320.6 3.5 reduce_sum.41
  324.1 8.6 %copy.54 = f32[8,128,1792]{2,1,0:T(8,128)} copy(f32[8,128,1792]{1,2,0:T(8,128)} %bitcast.10) | data formatting | bytes 14680064 | tf_op jit(solution)/shard_map/all_to_all | solution.py:128
  332.7 14.7 %fusion.1 = f32[1792,512,1]{1,0,2:T(8,128)S(1)} fusion(f32[1792]{0:T(1024)S(1)} %broadcast_multiply_fusion, f32[128,8,512]{0,2,1:T(8,128)S(1)} %copy-done.2, f32[512]{0:T(512)S(1)} %broadcast_multiply_fusion.1, f32[128,8,1792]{0,2,1:T(8,128)} %all-to-all-done), kind=kOutput, calls=%fused_computation.17 | convolution fusion | flops 11276648448 | bytes 13116416 | tf_op jit(solution)/shard_map/dot_general | solution.py:39
  348.6 26.1 %bitcast_add_fusion = f32[1024,1792]{1,0:T(8,128)} fusion(f32[8,128,1792]{2,1,0:T(8,128)S(1)} %copy-done, f32[224,8,4,128]{3,2,1,0:T(4,128)S(1)} %bitcast.169, f32[1792,512,1]{1,0,2:T(8,128)S(1)} %fusion.1, f32[128,1024]{1,0:T(8,128)S(1)} %fusion.74, f32[128,1024]{1,0:T(8,128)S(1)} %fusion.72, f32[128,1024]{1,0:T(8,128)S(1)} %copy-done.5, ...), kind=kOutput, calls=%fused_computation.14 | convolution fusion | flops 11279532032 | bytes 24117248 | tf_op jit(solution)/shard_map/dot_general | solution.py:51
  374.7 8.4 %copy.72 = f32[8,128,1792]{1,2,0:T(8,128)} copy(f32[8,128,1792]{2,1,0:T(8,128)} %bitcast.166) | data formatting | bytes 14680064 | tf_op jit(solution)/shard_map/all_to_all | solution.py:133
  383.1 5.1 all-to-all-start.3
  388.5 160.3 %all-to-all-done.3 = f32[8,128,1792]{1,2,0:T(8,128)} async-done(((f32[8,128,1792]{1,2,0:T(8,128)}), f32[8,128,1792]{1,2,0:T(8,128)}, u32[]{:S(2)}, u32[]{:S(2)}) %all-to-all-start.3) | async-done | bytes 7340064 | tf_op jit(solution)/shard_map/all_to_all | solution.py:133
  548.9 8.6 %copy.73 = f32[128,112,128]{2,0,1:T(8,128)} copy(f32[128,112,128]{0,2,1:T(8,128)} %bitcast.50) | data formatting | bytes 14680064 | tf_op jit(solution)/shard_map/reshape | solution.py:142
  557.5 5.9 %gather_fusion.3 = f32[64,128,128]{2,1,0:T(8,128)} fusion(f32[128,112,128]{2,0,1:T(8,128)} %copy.73, s32[1024]{0:T(1024)S(1)} %pad_clamp_fusion), kind=kCustom, calls=%fused_computation.11 | custom fusion | bytes 8388864 | tf_op jit(solution)/shard_map/jit(_take)/gather | solution.py:141
  563.4 5.6 copy.74
  569.0 7.5 %bitcast_select_fusion.1 = f32[128,8192]{0,1:T(8,128)} fusion(f32[128,64,128]{0,2,1:T(8,128)} %copy.74, pred[8192]{0:T(1024)(128)(4,1)S(1)} %broadcast_bitcast_fusion.2), kind=kLoop, calls=%fused_computation.19 | loop fusion | flops 1048576 | bytes 8396800 | tf_op jit(solution)/shard_map/jit(_take)/select_n | solution.py:141
  576.5 5.6 copy.75
  (134 shorter events, 42.2 us)
Async XLA Ops:
  9.4 11.4 %copy-start.8 = (s32[1,8,4]{1,2,0:T(4,128)S(1)}, s32[1,8,4]{1,2,0:T(4,128)}, u32[]{:S(2)}) copy-start(s32[1,8,4]{1,2,0:T(4,128)} %param.19) | copy-start | bytes 388
  12.9 8.0 %collective-permute-start = (f32[128,4,128]{2,0,1:T(8,128)}, f32[128,4,128]{2,0,1:T(8,128)S(1)}, u32[]{:S(2)}, u32[]{:S(2)}) collective-permute-start(f32[128,4,128]{2,0,1:T(8,128)} %get-tuple-element.45), channel_id=1, source_target_pairs={{3,0},{0,1},{1,2},{2,3},{7,4},{4,5},{5,6},{6,7},{11,8},{8,9},{9,10... | collective-permute-start | bytes 786440 | tf_op jit(solution)/shard_map/ppermute | solution.py:17
  17.1 7.4 %collective-permute-start.1 = (f32[128,4,128]{2,0,1:T(8,128)}, f32[128,4,128]{2,0,1:T(8,128)S(1)}, u32[]{:S(2)}, u32[]{:S(2)}) collective-permute-start(f32[128,4,128]{2,0,1:T(8,128)} %get-tuple-element.47), channel_id=1, source_target_pairs={{1,0},{2,1},{3,2},{0,3},{5,4},{6,5},{7,6},{4,7},{9,8},{10,9},{11,1... | collective-permute-start | bytes 786440 | tf_op jit(solution)/shard_map/ppermute | solution.py:17
  19.0 12.6 %collective-permute-start.4 = (f32[128,4,128]{2,0,1:T(8,128)S(1)}, f32[128,4,128]{2,0,1:T(8,128)S(1)}, u32[]{:S(2)}, u32[]{:S(2)}) collective-permute-start(f32[128,4,128]{2,0,1:T(8,128)S(1)} %get-tuple-element.44), channel_id=1, source_target_pairs={{3,0},{0,1},{1,2},{2,3},{7,4},{4,5},{5,6},{6,7},{11,8},{8,9},{9,10... | collective-permute-start | bytes 786440 | tf_op jit(solution)/shard_map/ppermute | solution.py:17
  19.7 11.9 %collective-permute-start.5 = (f32[128,4,128]{2,0,1:T(8,128)}, f32[128,4,128]{2,0,1:T(8,128)S(1)}, u32[]{:S(2)}, u32[]{:S(2)}) collective-permute-start(f32[128,4,128]{2,0,1:T(8,128)} %get-tuple-element.46), channel_id=1, source_target_pairs={{1,0},{2,1},{3,2},{0,3},{5,4},{6,5},{7,6},{4,7},{9,8},{10,9},{11,1... | collective-permute-start | bytes 786440 | tf_op jit(solution)/shard_map/ppermute | solution.py:17
  33.2 3.9 copy-start.3
  44.3 56.6 %all-to-all-start.1 = ((f32[128,8,512]{0,2,1:T(8,128)}), f32[128,8,512]{0,2,1:T(8,128)S(1)}, u32[]{:S(2)}, u32[]{:S(2)}) async-start(f32[128,8,512]{0,2,1:T(8,128)} %bitcast.175), calls=%async_computation.1 | async-start | bytes 4194304 | tf_op jit(solution)/shard_map/all_to_all | solution.py:108
  100.9 64.2 %copy-start.1 = (f32[128,8,512]{0,2,1:T(8,128)}, f32[128,8,512]{0,2,1:T(8,128)S(1)}, u32[]{:S(2)}) copy-start(f32[128,8,512]{0,2,1:T(8,128)S(1)} %all-to-all-done.1) | copy-start | bytes 6291460
  100.9 4.5 copy-start.10
  100.9 54.0 %all-to-all-start.2 = ((f32[128,8,512]{0,2,1:T(8,128)}), f32[128,8,512]{0,2,1:T(8,128)}, u32[]{:S(2)}, u32[]{:S(2)}) async-start(f32[128,8,512]{0,2,1:T(8,128)} %bitcast.174), calls=%async_computation.2 | async-start | bytes 4194304 | tf_op jit(solution)/shard_map/all_to_all | solution.py:109
  139.3 20.4 %copy-start.7 = (f32[4096]{0:T(1024)S(1)}, f32[4096]{0:T(1024)}, u32[]{:S(2)}) copy-start(f32[4096]{0:T(1024)} %param.17) | copy-start | bytes 49156
  139.3 23.8 %copy-start.9 = (s32[1,64,4]{1,2,0:T(4,128)S(1)}, s32[1,64,4]{1,2,0:T(4,128)}, u32[]{:S(2)}) copy-start(s32[1,64,4]{1,2,0:T(4,128)} %param.21) | copy-start | bytes 3076
  154.9 165.8 %all-to-all-start = ((f32[128,8,1792]{0,2,1:T(8,128)}), f32[128,8,1792]{0,2,1:T(8,128)}, u32[]{:S(2)}, u32[]{:S(2)}) async-start(f32[128,8,1792]{0,2,1:T(8,128)} %fusion), calls=%async_computation | async-start | bytes 14680064 | tf_op jit(solution)/shard_map/all_to_all | solution.py:128
  160.4 3.6 collective-permute-start.2
  161.0 3.3 collective-permute-start.3
  316.0 1.1 copy-start.4
  324.1 8.6 %copy-start.2 = (f32[128,8,512]{0,2,1:T(8,128)S(1)}, f32[128,8,512]{0,2,1:T(8,128)}, u32[]{:S(2)}) copy-start(f32[128,8,512]{0,2,1:T(8,128)} %copy-done.1) | copy-start | bytes 6291460
  332.7 15.3 %copy-start = (f32[8,128,1792]{2,1,0:T(8,128)S(1)}, f32[8,128,1792]{2,1,0:T(8,128)}, u32[]{:S(2)}) copy-start(f32[8,128,1792]{2,1,0:T(8,128)} %copy.54) | copy-start | bytes 22020100
  347.4 1.0 copy-start.5
  347.5 1.2 copy-start.6
  383.1 165.8 %all-to-all-start.3 = ((f32[8,128,1792]{1,2,0:T(8,128)}), f32[8,128,1792]{1,2,0:T(8,128)}, u32[]{:S(2)}, u32[]{:S(2)}) async-start(f32[8,128,1792]{1,2,0:T(8,128)} %copy.72), calls=%async_computation.3 | async-start | bytes 14680064 | tf_op jit(solution)/shard_map/all_to_all | solution.py:133
where the time goes:
time: 589 us; the launch traced here: 582 us
  waiting for transfers between devices  228 us (39%)
  other arithmetic  150 us (25%)
  local copies, waits for them, and re-layouts  116 us (20%)
  matrix products  56.8 us (10%)
  starting transfers between devices  28 us (5%)
    all_to_all x1, waiting for transfers between devices, body(): lax.all_to_all(result, 'member', split_axis=0, concat_axis=1, tiled=True)  160 us
    another operation x14, other arithmetic, local_solve(): factor = jnp.linalg.cholesky(cov_obs)  79 us
    all_to_all x1, waiting for transfers between devices, body(): lax.all_to_all(send_pred, 'member', split_axis=1, concat_axis=0, tiled=True)  46.2 us
    another operation x3, other arithmetic, local_solve(): weights = jax.scipy.linalg.cho_solve((factor, True), innovated.T)  40.2 us
    dot_general x1, matrix products, update(): lax.dot_general(weights, kalman_gain, (((0,), (1,)), ((), ())), precision...  26.1 us
    all_to_all x1, waiting for transfers between devices, body(): lax.all_to_all(send_innov, 'member', split_axis=1, concat_axis=0, tiled=T...  15.6 us
    gather x2, local copies, waits for them, and re-layouts, body(): outgoing = jnp.take(segment_roster, block_index.reshape(-1), axis=1)  14.9 us
    dot_general x1, matrix products, update(): lax.dot_general(centred, perturbed, (((0,), (0,)), ((), ())), precision=h...  14.7 us
  transfers between devices with their start and end apart: 10, of which 6 were waited for; matrix products, arithmetic and copies ran while one was open for 35% of the time, Pallas kernels for 0%

commit v1 on v0

v1 whole, which is shorter than its diff:
```python
import functools

import jax
import jax.numpy as jnp
from jax import lax
from jax.experimental import pallas as pl
from jax.experimental.pallas import tpu as pltpu
from jax.sharding import PartitionSpec as P

PIECE_LENGTH = 128
OBS_PER = 4
LOCAL = 512


highest = lax.Precision.HIGHEST
high = lax.Precision.HIGH


def shifted(block, axis, distance):
    count = lax.axis_size(axis)
    return lax.ppermute(block, axis, [(i, (i + distance) % count) for i in range(count)])


def pieces(start, count=1):
    return pl.ds(pl.multiple_of(start * PIECE_LENGTH, PIECE_LENGTH), count * PIECE_LENGTH)


def halo_kernel(ids_ref, expected_ref, innov_ref, after_ref, before_ref):
    count = ids_ref.shape[1]
    for side, out_ref in ((0, after_ref), (1, before_ref)):
        for k in range(count):
            source = pieces(ids_ref[side, k])
            out_ref[:, k * PIECE_LENGTH : (k + 1) * PIECE_LENGTH] = expected_ref[:, source]
            out_ref[:, (count + k) * PIECE_LENGTH : (count + k + 1) * PIECE_LENGTH] = innov_ref[:, source]


def halo_pack(ids, expected, innov):
    rows = expected.shape[0]
    shape = jax.ShapeDtypeStruct((rows, 2 * ids.shape[1] * PIECE_LENGTH), jnp.float32)
    return pl.pallas_call(
        halo_kernel,
        out_shape=(shape, shape),
        in_specs=[
            pl.BlockSpec(memory_space=pltpu.SMEM),
            pl.BlockSpec(memory_space=pltpu.VMEM),
            pl.BlockSpec(memory_space=pltpu.VMEM),
        ],
        out_specs=(pl.BlockSpec(memory_space=pltpu.VMEM),) * 2,
        name="halo_pack",
    )(ids, expected, innov)


def window_kernel(half, lists_ref, own_ref, before_ref, after_ref, out_ref):
    rows, width = own_ref.shape
    own_count = width // PIECE_LENGTH
    side = before_ref.shape[1] // (2 * PIECE_LENGTH)
    patches, per = lists_ref.shape

    @pl.loop(0, patches)
    def _(p):
        base = pl.multiple_of(p * rows, rows)
        for k in range(per):
            entry = lists_ref[p, k]
            target = (pl.ds(base, rows), slice(k * PIECE_LENGTH, (k + 1) * PIECE_LENGTH))

            @pl.when(entry < own_count)
            def _():
                out_ref[target] = own_ref[:, pieces(entry)]

            @pl.when((entry >= own_count) & (entry < own_count + side))
            def _():
                out_ref[target] = before_ref[:, pieces(entry - own_count + half * side)]

            @pl.when(entry >= own_count + side)
            def _():
                out_ref[target] = after_ref[:, pieces(entry - own_count - side + half * side)]


def window_pack(half, lists, own, before, after):
    rows = own.shape[0]
    patches, per = lists.shape
    return pl.pallas_call(
        functools.partial(window_kernel, half),
        out_shape=jax.ShapeDtypeStruct((patches * rows, per * PIECE_LENGTH), jnp.float32),
        in_specs=[pl.BlockSpec(memory_space=pltpu.SMEM)]
        + [pl.BlockSpec(memory_space=pltpu.VMEM)] * 3,
        out_specs=pl.BlockSpec(memory_space=pltpu.VMEM),
        name="window_pack",
    )(lists, own, before, after)


def to_owners(rows_by_owner):
    return lax.all_to_all(rows_by_owner, "member", split_axis=0, concat_axis=0, tiled=True)


def masked_gain(states, perturbed, cover_rows):
    realization_records, row_count = states.shape
    centred = states - jnp.mean(states, axis=0, keepdims=True)
    gain = lax.dot_general(
        centred,
        perturbed,
        (((0,), (0,)), ((), ())),
        precision=high,
        preferred_element_type=jnp.float32,
    ) / (realization_records - 1.0)
    cover = jnp.repeat(jnp.repeat(cover_rows, PIECE_LENGTH, axis=1), PIECE_LENGTH, axis=0)
    return gain * cover


def increment(weights, gain):
    return lax.dot_general(
        weights,
        gain,
        (((0,), (1,)), ((), ())),
        precision=high,
        preferred_element_type=jnp.float32,
    )


def body(
    background_realizations,
    realization_expected_data,
    departure_values,
    instrument_dispersion,
    window_piece_offsets,
    window_data_pieces,
    neighbor_piece_ids,
    coupling_indicator,
):
    groups = lax.axis_size("member")
    patch = lax.axis_index("member")
    rows, variable_total = background_realizations.shape
    segment_total = variable_total // PIECE_LENGTH
    per_device = segment_total // groups
    spread = (per_device - 1) // 2
    own_width = per_device * PIECE_LENGTH
    edge = spread * PIECE_LENGTH
    obs_count = realization_expected_data.shape[1] // PIECE_LENGTH
    lists = window_data_pieces[0]
    halo_ids = neighbor_piece_ids[0]

    after_send, before_send = halo_pack(halo_ids, realization_expected_data, departure_values)
    var_blocks = instrument_dispersion.reshape(obs_count, PIECE_LENGTH)
    from_before = shifted(after_send, "region", 1)
    from_after = shifted(before_send, "region", -1)
    var_before = shifted(jnp.take(var_blocks, halo_ids[0], axis=0), "region", 1)
    var_after = shifted(jnp.take(var_blocks, halo_ids[1], axis=0), "region", -1)
    var_ext = jnp.concatenate([var_blocks, var_before, var_after], axis=0)

    expected = to_owners(
        window_pack(0, lists, realization_expected_data, from_before, from_after)
    )
    send_innov = window_pack(1, lists, departure_values, from_before, from_after)
    send_states = (
        background_realizations.reshape(rows, groups, own_width)
        .transpose(1, 0, 2)
        .reshape(groups * rows, own_width)
    )
    arrived = to_owners(jnp.concatenate([send_innov, send_states], axis=1))
    innovated = arrived[:, :LOCAL]
    states = arrived[:, LOCAL:]
    members = states.shape[0]

    own_list = lax.dynamic_index_in_dim(lists, patch, 0, keepdims=False)
    variance = jnp.take(var_ext, own_list, axis=0).reshape(LOCAL)
    perturbed = expected - jnp.mean(expected, axis=0, keepdims=True)
    cov_obs = jnp.dot(
        perturbed.T, perturbed, precision=highest, preferred_element_type=jnp.float32
    ) / (members - 1.0)
    cov_obs = cov_obs + jnp.diag(variance)
    factor = jnp.linalg.cholesky(cov_obs)
    weights = jax.scipy.linalg.cho_solve((factor, True), innovated.T)

    up = [(i, i + 1) for i in range(groups - 1)]
    down = [(i + 1, i) for i in range(groups - 1)]
    low_states = lax.ppermute(states[:, own_width - edge :], "member", up)
    high_states = lax.ppermute(states[:, :edge], "member", down)
    edge_states = jnp.concatenate([low_states, high_states], axis=1)

    cover_all = coupling_indicator[0].astype(jnp.float32)
    first = patch * per_device
    own_cover = lax.dynamic_slice_in_dim(cover_all, first, per_device, axis=0)
    low_ids = jnp.maximum(first - spread + jnp.arange(spread), 0)
    high_ids = jnp.minimum(first + per_device + jnp.arange(spread), segment_total - 1)
    edge_cover = jnp.take(cover_all, jnp.concatenate([low_ids, high_ids]), axis=0)

    own_gain = masked_gain(states, perturbed, own_cover)
    edge_gain = masked_gain(edge_states, perturbed, edge_cover)
    edge_inc = increment(weights, edge_gain)
    inc_high = lax.ppermute(edge_inc[:, :edge], "member", down)
    inc_low = lax.ppermute(edge_inc[:, edge:], "member", up)
    own_inc = increment(weights, own_gain)
    bounds = lax.dynamic_slice_in_dim(window_piece_offsets[0], patch, 2) - first
    block = jnp.arange(own_width) // PIECE_LENGTH
    from_low = (block < bounds[0])[None, :edge]
    from_high = (block >= bounds[1])[None, own_width - edge :]
    result = states + jnp.concatenate(
        [
            jnp.where(from_low, inc_low, own_inc[:, :edge]),
            own_inc[:, edge : own_width - edge],
            jnp.where(from_high, inc_high, own_inc[:, own_width - edge :]),
        ],
        axis=1,
    )
    returned = to_owners(result)
    return (
        returned.reshape(groups, rows, own_width).transpose(1, 0, 2).reshape(rows, variable_total)
    )


def solution(mesh):
    return jax.shard_map(
        body,
        mesh=mesh,
        in_specs=(
            P("member", "region"),
            P("member", "region"),
            P("member", "region"),
            P("region"),
            P("region", None),
            P("region", None, None),
            P("region", None, None),
            P("region", None, None),
        ),
        out_specs=P("member", "region"),
        check_vma=False,
    )
```

time: 589 us -> 509 us (0.86)
  blocking collectives: 0 us -> 101 us
  local copies, waits for them, and re-layouts: 116 us -> 34.9 us
  waiting for transfers between devices: 228 us -> 147 us
  other arithmetic: 150 us -> 137 us
  Pallas kernels: 0 us -> 11.4 us
  matrix products: 56.8 us -> 45.5 us
    all_to_all x4 -> x2, waiting for transfers between devices: 224 us -> 34.3 us  [to_owners(): lax.all_to_all(rows_by_owner, 'member', split_axis=0, concat_axis=0, tile...]
    ppermute x6 -> x8, waiting for transfers between devices: 3.83 us -> 112 us  [the longest x1 51.7 us: body(): low_states = lax.ppermute(states[:, own_width - edge:], 'member', up)]
    all_to_all x0 -> x1, blocking collectives: none -> 101 us  [to_owners(): lax.all_to_all(rows_by_owner, 'member', split_axis=0, concat_axis=0, tile...]
    gather x13 -> x3, local copies, waits for them, and re-layouts: 41.2 us -> 1.67 us  [the longest x1 0.56 us: body(): var_after = shifted(jnp.take(var_blocks, halo_ids[1], axis=0), 'region', -1)]
    all_to_all x4 -> x0, local copies, waits for them, and re-layouts: 21.8 us -> none  [the longest x1 8.6 us: body(): lax.all_to_all(outgoing, 'member', split_axis=1, concat_axis=0, tiled=True)]
    select_n x12 -> x5, other arithmetic: 20.9 us -> 0.6 us  [the longest x1 0.31 us: body(): jnp.where(from_low, inc_low, own_inc[:, :edge])]
    dot_general x3 -> x5, matrix products: 44.5 us -> 25.7 us  [the longest x2 12.1 us: increment(): lax.dot_general(weights, gain, (((0,), (1,)), ((), ())), precision=high,...]
    select_n x3 -> x0, local copies, waits for them, and re-layouts: 11.4 us -> none  [the longest x1 5.59 us: body(): jnp.take(returned.reshape(neighbor_realization_records, groups * patch_mo...]
  transfers between devices with their start and end apart: 10 -> 10, of which waited for: 6 -> 6; matrix products, arithmetic and copies ran while one was open for 35% -> 38% of each run, Pallas kernels for 0% -> 1%
where the time goes in v1:
time: 509 us; the launch traced here: 505 us
  waiting for transfers between devices  147 us (29%)
  other arithmetic  137 us (27%)
  blocking collectives  101 us (20%)
  matrix products  45.5 us (9%)
  local copies, waits for them, and re-layouts  34.9 us (7%)
  starting transfers between devices  25 us (5%)
  Pallas kernels  11.4 us (2%)
    all_to_all x1, blocking collectives, to_owners(): lax.all_to_all(rows_by_owner, 'member', split_axis=0, concat_axis=0, tile...  101 us
    another operation x14, other arithmetic, body(): factor = jnp.linalg.cholesky(cov_obs)  78.6 us
    ppermute x1, waiting for transfers between devices, body(): low_states = lax.ppermute(states[:, own_width - edge:], 'member', up)  51.7 us
    ppermute x1, waiting for transfers between devices, body(): inc_low = lax.ppermute(edge_inc[:, edge:], 'member', up)  47.3 us
    another operation x3, other arithmetic, body(): weights = jax.scipy.linalg.cho_solve((factor, True), innovated.T)  41.3 us
    all_to_all x2, waiting for transfers between devices, to_owners(): lax.all_to_all(rows_by_owner, 'member', split_axis=0, concat_axis=0, tile...  34.3 us
    another operation x12, local copies, waits for them, and re-layouts  14 us
    another operation x14, matrix products, body(): weights = jax.scipy.linalg.cho_solve((factor, True), innovated.T)  13.9 us
  transfers between devices with their start and end apart: 10, of which 6 were waited for; matrix products, arithmetic and copies ran while one was open for 38% of the time, Pallas kernels for 1%

profile of v1, /device:TPU:0, one launch (start us, length us, event | category | flops | bytes accessed | tf_op | source)
XLA Modules:
  0.0 505.4 jit_solution(17780043820589452511)
XLA Ops:
  0.0 3.4 halo_pack.1
  3.9 1.9 collective-permute-start.1
  6.4 9.4 %collective-permute-done.before_ref = f32[128,1024]{1,0:T(8,128)S(1)} collective-permute-done((f32[128,1024]{1,0:T(8,128)}, f32[128,1024]{1,0:T(8,128)S(1)}, u32[]{:S(2)}, u32[]{:S(2)}) %collective-permute-start) | collective-permute-done | bytes 524320 | tf_op jit(solution)/shard_map/ppermute | solution.py:21
  15.8 2.6 collective-permute-done.1.after_ref
  19.2 4.0 window_pack.3
  23.2 5.8 %all-to-all-start.1 = ((f32[8,128,512]{2,1,0:T(8,128)}), f32[8,128,512]{2,1,0:T(8,128)S(1)}, u32[]{:S(2)}, u32[]{:S(2)}) async-start(f32[8,128,512]{2,1,0:T(8,128)} %bitcast.120), calls=%async_computation.1 | async-start | bytes 4194304 | tf_op jit(solution)/shard_map/all_to_all | solution.py:93
  29.1 4.8 copy.39
  33.9 4.0 window_pack.2
  37.9 6.0 %pad_maximum_fusion = f32[8,128,1536]{2,1,0:T(8,128)} fusion(f32[8,128,1024]{2,1,0:T(8,128)} %bitcast.117, f32[8,128,512]{2,1,0:T(8,128)} %bitcast.121), kind=kLoop, calls=%fused_computation.6 | loop fusion | flops 1572864 | bytes 12582912 | tf_op jit(solution)/shard_map/concatenate | solution.py:159
  43.8 34.3 %all-to-all-done.1 = f32[8,128,512]{2,1,0:T(8,128)S(1)} async-done(((f32[8,128,512]{2,1,0:T(8,128)}), f32[8,128,512]{2,1,0:T(8,128)S(1)}, u32[]{:S(2)}, u32[]{:S(2)}) %all-to-all-start.1) | async-done | bytes 2097184 | tf_op jit(solution)/shard_map/all_to_all | solution.py:93
  78.2 4.8 all-to-all-start
  88.3 3.6 fusion.28
  93.2 1.5 add_multiply_fusion
  95.6 11.7 %cholesky.103 = f32[128,128]{1,0:T(8,128)S(1)} custom-call(f32[128,128]{1,0:T(8,128)S(1)} %cholesky.263), custom_call_target="Cholesky" | custom-call | tf_op jit(solution)/shard_map/jit(cholesky)/cholesky | solution.py:171
  107.5 9.8 %custom-call.34 = f32[1,128,128]{1,2,0:T(8,128)S(1)} custom-call(f32[1,128,128]{2,1,0:T(8,128)S(1)} %get-tuple-element.47), custom_call_target="InvertDiagBlocksLowerTriangular" | custom-call | tf_op jit(solution)/shard_map/jit(cholesky)/cholesky | solution.py:171
  119.9 11.9 %cholesky.215 = f32[128,128]{1,0:T(8,128)S(1)} custom-call(f32[128,128]{1,0:T(8,128)S(1)} %cholesky.267), custom_call_target="Cholesky" | custom-call | tf_op jit(solution)/shard_map/jit(cholesky)/cholesky | solution.py:171
  131.8 9.8 %custom-call.35 = f32[1,128,128]{1,2,0:T(8,128)S(1)} custom-call(f32[1,128,128]{2,1,0:T(8,128)S(1)} %get-tuple-element.44), custom_call_target="InvertDiagBlocksLowerTriangular" | custom-call | tf_op jit(solution)/shard_map/jit(cholesky)/cholesky | solution.py:171
  143.2 11.7 %cholesky.236 = f32[128,128]{1,0:T(8,128)S(1)} custom-call(f32[128,128]{1,0:T(8,128)S(1)} %cholesky.272), custom_call_target="Cholesky" | custom-call | tf_op jit(solution)/shard_map/jit(cholesky)/cholesky | solution.py:171
  154.9 9.8 %custom-call.36 = f32[1,128,128]{1,2,0:T(8,128)S(1)} custom-call(f32[1,128,128]{2,1,0:T(8,128)S(1)} %get-tuple-element.41), custom_call_target="InvertDiagBlocksLowerTriangular" | custom-call | tf_op jit(solution)/shard_map/jit(cholesky)/cholesky | solution.py:171
  165.0 1.6 convolution_subtract_fusion.6
  166.6 11.7 %cholesky.253 = f32[128,128]{1,0:T(8,128)S(1)} custom-call(f32[128,128]{1,0:T(8,128)S(1)} %convolution_subtract_fusion.6), custom_call_target="Cholesky" | custom-call | tf_op jit(solution)/shard_map/jit(cholesky)/cholesky | solution.py:171
  184.0 14.0 %while.1 = (s32[]{:T(128)}, f32[512,512]{1,0:T(8,128)}, s32[4,2]{0,1:T(2,128)S(1)}, f32[4,128,128]{2,1,0:T(8,128)}, s32[]{:T(128)}) while((s32[]{:T(128)}, f32[512,512]{1,0:T(8,128)}, s32[4,2]{0,1:T(2,128)S(1)}, f32[4,128,128]{2,1,0:T(8,128)}, s32[]{:T(128)}) %tuple.39), condition=%wide.while_cond, body=%wide.while_body.sunk | while | flops 2 | bytes 132205 | solution.py:172
  184.7 2.9 bitcast_dynamic-update-slice_fusion.2
  188.2 2.9 bitcast_dynamic-update-slice_fusion.2
  191.7 2.9 bitcast_dynamic-update-slice_fusion.2
  195.2 2.9 bitcast_dynamic-update-slice_fusion.2
  198.1 40.1 %custom-call.37 = f32[4,128,128]{1,2,0:T(8,128)S(1)} custom-call(f32[4,128,128]{2,1,0:T(8,128)} %get-tuple-element.17), custom_call_target="InvertDiagBlocksLowerTriangular" | custom-call | tf_op jit(solution)/shard_map/jit(_cho_solve)/triangular_solve | solution.py:172
  238.2 1.6 bitcast_subtract_fusion
  239.8 2.1 fusion.89
  241.9 1.9 slice_bitcast_fusion
  243.8 3.9 collective-permute-start.4
  247.7 1.5 collective-permute-start.5
  251.5 1.8 convolution_subtract_fusion.1
  253.9 2.7 fusion.34
  261.6 1.6 fusion.65
  263.2 51.7 %collective-permute-done.4 = f32[1024,384]{1,0:T(8,128)S(1)} collective-permute-done((f32[1024,384]{1,0:T(8,128)S(1)}, f32[1024,384]{1,0:T(8,128)S(1)}, u32[]{:S(2)}, u32[]{:S(2)}) %collective-permute-start.4) | collective-permute-done | bytes 1572896 | tf_op jit(solution)/shard_map/ppermute | solution.py:176
  315.5 4.4 bitcast_multiply_fusion.1
  319.9 5.2 %fusion.38 = f32[1024,768]{1,0:T(8,128)S(1)} fusion(f32[768,512]{1,0:T(8,128)S(1)} %bitcast_multiply_fusion.1, f32[128,1024]{1,0:T(8,128)S(1)} %copy-done.2, f32[128,1024]{1,0:T(8,128)S(1)} %copy-done.5, f32[128,1024]{1,0:T(8,128)S(1)} %copy-done.8, f32[128,1024]{1,0:T(8,128)S(1)} %copy-done.10), kind=kOutput, calls=%fused_computation.47 | convolution fusion | flops 2417491968 | bytes 6815744 | tf_op jit(solution)/shard_map/dot_general | solution.py:111
  325.2 1.9 fusion.90
  327.1 4.5 collective-permute-start.6
  331.6 1.5 collective-permute-start.7
  335.4 2.6 slice_reduce_fusion
  338.2 5.7 %bitcast_multiply_fusion = f32[1024,512]{1,0:T(8,128)S(1)} fusion(f32[1024,512]{1,0:T(8,128)S(1)} %copy-done, f32[1024,1536]{1,0:T(8,128)} %bitcast.4, f32[1024]{0:T(1024)S(1)} %broadcast_multiply_fusion, f32[8,512]{1,0:T(8,128)S(1)} %broadcast_bitcast_fusion), kind=kOutput, calls=%fused_computation.17 | convolution fusion | flops 3223322624 | bytes 8409088 | tf_op jit(solution)/shard_map/dot_general | solution.py:99
  344.0 6.9 %fusion.37 = f32[1024,1024]{1,0:T(8,128)S(1)} fusion(f32[1024,512]{1,0:T(8,128)S(1)} %bitcast_multiply_fusion, f32[128,1024]{1,0:T(8,128)S(1)} %copy-done.3, f32[128,1024]{1,0:T(8,128)S(1)} %copy-done.6, f32[128,1024]{1,0:T(8,128)S(1)} %copy-done.9, f32[128,1024]{1,0:T(8,128)S(1)} %copy-done.11), kind=kOutput, calls=%fused_computation.46 | convolution fusion | flops 3222798336 | bytes 8388608 | tf_op jit(solution)/shard_map/dot_general | solution.py:111
  351.0 47.3 %collective-permute-done.6 = f32[1024,384]{1,0:T(8,128)S(1)} collective-permute-done((f32[1024,384]{1,0:T(8,128)}, f32[1024,384]{1,0:T(8,128)S(1)}, u32[]{:S(2)}, u32[]{:S(2)}) %collective-permute-start.6) | collective-permute-done | bytes 1572896 | tf_op jit(solution)/shard_map/ppermute | solution.py:191
  398.6 2.9 maximum_add_fusion
  401.5 101.3 %all_to_all.30 = f32[8,128,1024]{2,1,0:T(8,128)S(1)} all-to-all(f32[8,128,1024]{2,1,0:T(8,128)S(1)} %bitcast.118), channel_id=1, replica_groups=mesh['member'=8,'region'=4] {'member'}, dimensions={0} | all-to-all | bytes 8388608 | tf_op jit(solution)/shard_map/all_to_all | solution.py:93
  502.8 2.3 copy.35
  (134 shorter events, 30.8 us)
Async XLA Ops:
  0.0 5.8 %copy-start.17 = (s32[1,8,4]{1,2,0:T(4,128)S(1)}, s32[1,8,4]{1,2,0:T(4,128)}, u32[]{:S(2)}) copy-start(s32[1,8,4]{1,2,0:T(4,128)} %param.15) | copy-start | bytes 388
  3.4 12.5 %collective-permute-start = (f32[128,1024]{1,0:T(8,128)}, f32[128,1024]{1,0:T(8,128)S(1)}, u32[]{:S(2)}, u32[]{:S(2)}) collective-permute-start(f32[128,1024]{1,0:T(8,128)} %get-tuple-element.8), channel_id=1, source_target_pairs={{0,1},{1,2},{2,3},{3,0},{4,5},{5,6},{6,7},{7,4},{8,9},{9,10},{10,1... | collective-permute-start | bytes 1572872 | tf_op jit(solution)/shard_map/ppermute | solution.py:21
  3.9 14.5 %collective-permute-start.1 = (f32[128,1024]{1,0:T(8,128)}, f32[128,1024]{1,0:T(8,128)S(1)}, u32[]{:S(2)}, u32[]{:S(2)}) collective-permute-start(f32[128,1024]{1,0:T(8,128)} %get-tuple-element.9), channel_id=1, source_target_pairs={{0,3},{1,0},{2,1},{3,2},{4,7},{5,4},{6,5},{7,6},{8,11},{9,8},{10,9... | collective-permute-start | bytes 1572872 | tf_op jit(solution)/shard_map/ppermute | solution.py:21
  15.8 2.6 copy-start.14
  18.4 0.8 copy-start.15
  23.2 54.9 %all-to-all-start.1 = ((f32[8,128,512]{2,1,0:T(8,128)}), f32[8,128,512]{2,1,0:T(8,128)S(1)}, u32[]{:S(2)}, u32[]{:S(2)}) async-start(f32[8,128,512]{2,1,0:T(8,128)} %bitcast.120), calls=%async_computation.1 | async-start | bytes 4194304 | tf_op jit(solution)/shard_map/all_to_all | solution.py:93
  43.8 39.1 %copy-start.18 = (s32[1,2,4]{2,1,0:T(2,128)S(1)}, s32[1,2,4]{2,1,0:T(2,128)}, u32[]{:S(2)}) copy-start(s32[1,2,4]{2,1,0:T(2,128)} %param.16) | copy-start | bytes 100
  43.8 39.2 %copy-start.16 = (f32[4096]{0:T(1024)S(1)}, f32[4096]{0:T(1024)}, u32[]{:S(2)}) copy-start(f32[4096]{0:T(1024)} %param.13) | copy-start | bytes 49156
  43.8 41.1 %copy-start.19 = (s32[1,64,4]{1,2,0:T(4,128)S(1)}, s32[1,64,4]{1,2,0:T(4,128)}, u32[]{:S(2)}) copy-start(s32[1,64,4]{1,2,0:T(4,128)} %param.17) | copy-start | bytes 3076
  78.2 161.6 %all-to-all-start = ((f32[8,128,1536]{2,1,0:T(8,128)}), f32[8,128,1536]{2,1,0:T(8,128)}, u32[]{:S(2)}, u32[]{:S(2)}) async-start(f32[8,128,1536]{2,1,0:T(8,128)} %pad_maximum_fusion), calls=%async_computation | async-start | bytes 12582912 | tf_op jit(solution)/shard_map/all_to_all | solution.py:93
  83.6 2.5 collective-permute-start.3
  84.3 3.2 collective-permute-start.2
  94.7 1.0 copy-start.13
  241.9 7.9 %copy-start.12 = (f32[512,512]{1,0:T(8,128)S(1)}, f32[512,512]{1,0:T(8,128)}, u32[]{:S(2)}) copy-start(f32[512,512]{1,0:T(8,128)} %get-tuple-element.111) | copy-start | bytes 3145732
  243.8 71.2 %collective-permute-start.4 = (f32[1024,384]{1,0:T(8,128)S(1)}, f32[1024,384]{1,0:T(8,128)S(1)}, u32[]{:S(2)}, u32[]{:S(2)}) collective-permute-start(f32[1024,384]{1,0:T(8,128)S(1)} %get-tuple-element.33), channel_id=1, source_target_pairs={{0,4},{4,8},{8,12},{12,16},{16,20},{20,24},{24,28},{1,5},{5,9},{9,... | collective-permute-start | bytes 4718600 | tf_op jit(solution)/shard_map/ppermute | solution.py:176
  247.7 67.4 %collective-permute-start.5 = (f32[1024,384]{1,0:T(8,128)S(1)}, f32[1024,384]{1,0:T(8,128)S(1)}, u32[]{:S(2)}, u32[]{:S(2)}) collective-permute-start(f32[1024,384]{1,0:T(8,128)S(1)} %get-tuple-element.32), channel_id=1, source_target_pairs={{4,0},{8,4},{12,8},{16,12},{20,16},{24,20},{28,24},{5,1},{9,5},{13... | collective-permute-start | bytes 4718600 | tf_op jit(solution)/shard_map/ppermute | solution.py:177
  257.9 2.6 copy-start.1
  259.1 2.5 copy-start.4
  260.4 54.6 %copy-start.7 = (f32[128,1024]{1,0:T(8,128)}, f32[128,1024]{1,0:T(8,128)S(1)}, u32[]{:S(2)}) copy-start(f32[128,1024]{1,0:T(8,128)S(1)} %fusion.66) | copy-start | bytes 1572868
  315.5 4.4 copy-start.2
  315.5 4.4 copy-start.5
  315.5 4.4 copy-start.8
  315.5 4.4 copy-start.10
  325.2 8.1 %copy-start.20 = (s32[1,9]{1,0:T(1,128)S(1)}, s32[1,9]{1,0:T(1,128)}, u32[]{:S(2)}) copy-start(s32[1,9]{1,0:T(1,128)} %param.14) | copy-start | bytes 112
  327.1 71.2 %collective-permute-start.6 = (f32[1024,384]{1,0:T(8,128)}, f32[1024,384]{1,0:T(8,128)S(1)}, u32[]{:S(2)}, u32[]{:S(2)}) collective-permute-start(f32[1024,384]{1,0:T(8,128)} %get-tuple-element.36), channel_id=1, source_target_pairs={{0,4},{4,8},{8,12},{12,16},{16,20},{20,24},{24,28},{1,5},{5,9},{9,... | collective-permute-start | bytes 4718600 | tf_op jit(solution)/shard_map/ppermute | solution.py:191
  331.6 66.7 %collective-permute-start.7 = (f32[1024,384]{1,0:T(8,128)}, f32[1024,384]{1,0:T(8,128)S(1)}, u32[]{:S(2)}, u32[]{:S(2)}) collective-permute-start(f32[1024,384]{1,0:T(8,128)} %get-tuple-element.37), channel_id=1, source_target_pairs={{4,0},{8,4},{12,8},{16,12},{20,16},{24,20},{28,24},{5,1},{9,5},{13... | collective-permute-start | bytes 4718600 | tf_op jit(solution)/shard_map/ppermute | solution.py:190
  335.4 2.9 copy-start
  338.2 5.7 %copy-start.3 = (f32[128,1024]{1,0:T(8,128)S(1)}, f32[128,1024]{1,0:T(8,128)}, u32[]{:S(2)}) copy-start(f32[128,1024]{1,0:T(8,128)} %copy-done.1) | copy-start | bytes 1572868
  338.2 5.7 %copy-start.6 = (f32[128,1024]{1,0:T(8,128)S(1)}, f32[128,1024]{1,0:T(8,128)}, u32[]{:S(2)}) copy-start(f32[128,1024]{1,0:T(8,128)} %copy-done.4) | copy-start | bytes 1572868
  338.2 5.7 %copy-start.9 = (f32[128,1024]{1,0:T(8,128)S(1)}, f32[128,1024]{1,0:T(8,128)}, u32[]{:S(2)}) copy-start(f32[128,1024]{1,0:T(8,128)} %copy-done.7) | copy-start | bytes 1572868
  338.2 5.7 %copy-start.11 = (f32[128,1024]{1,0:T(8,128)S(1)}, f32[128,1024]{1,0:T(8,128)}, u32[]{:S(2)}) copy-start(f32[128,1024]{1,0:T(8,128)} %fusion.65) | copy-start | bytes 1572868

commit v2 on v1

--- a/solution.py
+++ b/solution.py
@@ -93,6 +93,59 @@
     return lax.all_to_all(rows_by_owner, "member", split_axis=0, concat_axis=0, tiled=True)
 
 
+def snake(index, row):
+    return index + (index // row) % 2 * (row - 1 - 2 * (index % row))
+
+
+def split_kernel(in_ref, first_ref, second_ref):
+    half = first_ref.shape[1]
+    first_ref[...] = in_ref[:, :half]
+    second_ref[...] = in_ref[:, half:]
+
+
+def state_pack(background, groups, row, half):
+    rows, total = background.shape
+    width = total // groups
+    return pl.pallas_call(
+        split_kernel,
+        grid=(groups,),
+        out_shape=(
+            jax.ShapeDtypeStruct((groups * rows, half), jnp.float32),
+            jax.ShapeDtypeStruct((groups * rows, width - half), jnp.float32),
+        ),
+        in_specs=[pl.BlockSpec((rows, width), lambda i: (0, snake(i, row)))],
+        out_specs=(
+            pl.BlockSpec((rows, half), lambda i: (i, 0)),
+            pl.BlockSpec((rows, width - half), lambda i: (i, 0)),
+        ),
+        name="state_pack",
+    )(background)
+
+
+def join_kernel(edge, centre_ref, sides_ref, out_ref):
+    width = out_ref.shape[1]
+    out_ref[:, :edge] = sides_ref[:, :edge]
+    out_ref[:, edge : width - edge] = centre_ref[...]
+    out_ref[:, width - edge :] = sides_ref[:, edge:]
+
+
+def state_join(centre, sides, groups, row):
+    rows = centre.shape[0] // groups
+    edge = sides.shape[1] // 2
+    width = centre.shape[1] + 2 * edge
+    return pl.pallas_call(
+        functools.partial(join_kernel, edge),
+        grid=(groups,),
+        out_shape=jax.ShapeDtypeStruct((rows, groups * width), jnp.float32),
+        in_specs=[
+            pl.BlockSpec((rows, width - 2 * edge), lambda i: (i, 0)),
+            pl.BlockSpec((rows, 2 * edge), lambda i: (i, 0)),
+        ],
+        out_specs=pl.BlockSpec((rows, width), lambda i: (0, snake(i, row))),
+        name="state_join",
+    )(centre, sides)
+
+
 def masked_gain(states, perturbed, cover_rows):
     realization_records, row_count = states.shape
     centred = states - jnp.mean(states, axis=0, keepdims=True)
@@ -107,17 +160,55 @@
     return gain * cover
 
 
-def increment(weights, gain):
+def times_transposed(left, right, precision=high):
     return lax.dot_general(
-        weights,
-        gain,
-        (((0,), (1,)), ((), ())),
-        precision=high,
+        left,
+        right,
+        (((1,), (1,)), ((), ())),
+        precision=precision,
         preferred_element_type=jnp.float32,
     )
 
 
+def factor_block(block):
+    lower = jnp.linalg.cholesky(block)
+    return lax.linalg.triangular_solve(
+        lower, jnp.eye(PIECE_LENGTH, dtype=jnp.float32), left_side=True, lower=True
+    )
+
+
+def factor_step(trailing):
+    inverse = factor_block(trailing[:PIECE_LENGTH, :PIECE_LENGTH])
+    panel = times_transposed(trailing[PIECE_LENGTH:, :PIECE_LENGTH], inverse, highest)
+    rest = trailing[PIECE_LENGTH:, PIECE_LENGTH:] - times_transposed(panel, panel, highest)
+    return inverse, panel, rest
+
+
+def solve_rows(inverses, panels, innovated):
+    count = len(inverses)
+    rest = innovated
+    forward = []
+    for k in range(count):
+        part = times_transposed(rest[:, :PIECE_LENGTH], inverses[k], highest)
+        forward.append(part)
+        if k + 1 < count:
+            rest = rest[:, PIECE_LENGTH:] - times_transposed(part, panels[k], highest)
+    done = None
+    for k in reversed(range(count)):
+        part = forward[k]
+        if done is not None:
+            part = part - jnp.dot(
+                done, panels[k], precision=highest, preferred_element_type=jnp.float32
+            )
+        part = jnp.dot(
+            part, inverses[k], precision=highest, preferred_element_type=jnp.float32
+        )
+        done = part if done is None else jnp.concatenate([part, done], axis=1)
+    return done
+
+
 def body(
+    row,
     background_realizations,
     realization_expected_data,
     departure_values,
@@ -128,16 +219,23 @@
     coupling_indicator,
 ):
     groups = lax.axis_size("member")
-    patch = lax.axis_index("member")
+    patch = snake(lax.axis_index("member"), row)
     rows, variable_total = background_realizations.shape
     segment_total = variable_total // PIECE_LENGTH
     per_device = segment_total // groups
     spread = (per_device - 1) // 2
     own_width = per_device * PIECE_LENGTH
+    half = per_device // 2 * PIECE_LENGTH
     edge = spread * PIECE_LENGTH
     obs_count = realization_expected_data.shape[1] // PIECE_LENGTH
     lists = window_data_pieces[0]
+    sorted_lists = jnp.stack([lists[snake(i, row)] for i in range(groups)])
     halo_ids = neighbor_piece_ids[0]
+    up = [(snake(p, row), snake(p + 1, row)) for p in range(groups - 1)]
+    down = [(after, before) for before, after in up]
+
+    send_first, send_second = state_pack(background_realizations, groups, row, half)
+    first_states = to_owners(send_first)
 
     after_send, before_send = halo_pack(halo_ids, realization_expected_data, departure_values)
     var_blocks = instrument_dispersion.reshape(obs_count, PIECE_LENGTH)
@@ -146,71 +244,102 @@
     var_before = shifted(jnp.take(var_blocks, halo_ids[0], axis=0), "region", 1)
     var_after = shifted(jnp.take(var_blocks, halo_ids[1], axis=0), "region", -1)
     var_ext = jnp.concatenate([var_blocks, var_before, var_after], axis=0)
-
-    expected = to_owners(
-        window_pack(0, lists, realization_expected_data, from_before, from_after)
-    )
-    send_innov = window_pack(1, lists, departure_values, from_before, from_after)
-    send_states = (
-        background_realizations.reshape(rows, groups, own_width)
-        .transpose(1, 0, 2)
-        .reshape(groups * rows, own_width)
-    )
-    arrived = to_owners(jnp.concatenate([send_innov, send_states], axis=1))
-    innovated = arrived[:, :LOCAL]
-    states = arrived[:, LOCAL:]
-    members = states.shape[0]
-
     own_list = lax.dynamic_index_in_dim(lists, patch, 0, keepdims=False)
     variance = jnp.take(var_ext, own_list, axis=0).reshape(LOCAL)
+
+    send_expected = window_pack(
+        0, sorted_lists, realization_expected_data, from_before, from_after
+    )
+    send_innov = window_pack(1, sorted_lists, departure_values, from_before, from_after)
+    first_states, send_expected, send_innov, variance = lax.optimization_barrier(
+        (first_states, send_expected, send_innov, variance)
+    )
+    expected = to_owners(send_expected)
+    expected, send_second, first_states = lax.optimization_barrier(
+        (expected, send_second, first_states)
+    )
+    second_states = to_owners(send_second)
+    high_states = lax.ppermute(first_states[:, :edge], "member", down)
+    members = first_states.shape[0]
+
     perturbed = expected - jnp.mean(expected, axis=0, keepdims=True)
     cov_obs = jnp.dot(
         perturbed.T, perturbed, precision=highest, preferred_element_type=jnp.float32
     ) / (members - 1.0)
-    cov_obs = cov_obs + jnp.diag(variance)
-    factor = jnp.linalg.cholesky(cov_obs)
-    weights = jax.scipy.linalg.cho_solve((factor, True), innovated.T)
-
-    up = [(i, i + 1) for i in range(groups - 1)]
-    down = [(i + 1, i) for i in range(groups - 1)]
-    low_states = lax.ppermute(states[:, own_width - edge :], "member", up)
-    high_states = lax.ppermute(states[:, :edge], "member", down)
-    edge_states = jnp.concatenate([low_states, high_states], axis=1)
+    trailing = cov_obs + jnp.diag(variance)
+    inverses, panels = [], []
+    for k in range(OBS_PER):
+        if k == OBS_PER // 2:
+            trailing, second_states, send_innov = lax.optimization_barrier(
+                (trailing, second_states, send_innov)
+            )
+            innovated = to_owners(send_innov)
+            low_states = lax.ppermute(
+                second_states[:, own_width - half - edge :], "member", up
+            )
+        if k + 1 < OBS_PER:
+            inverse, panel, trailing = factor_step(trailing)
+            panels.append(panel)
+        else:
+            inverse = factor_block(trailing)
+        inverses.append(inverse)
+    inverses[-1], innovated = lax.optimization_barrier((inverses[-1], innovated))
+    weights = solve_rows(inverses, panels, innovated)
 
     cover_all = coupling_indicator[0].astype(jnp.float32)
     first = patch * per_device
-    own_cover = lax.dynamic_slice_in_dim(cover_all, first, per_device, axis=0)
-    low_ids = jnp.maximum(first - spread + jnp.arange(spread), 0)
-    high_ids = jnp.minimum(first + per_device + jnp.arange(spread), segment_total - 1)
-    edge_cover = jnp.take(cover_all, jnp.concatenate([low_ids, high_ids]), axis=0)
-
-    own_gain = masked_gain(states, perturbed, own_cover)
-    edge_gain = masked_gain(edge_states, perturbed, edge_cover)
-    edge_inc = increment(weights, edge_gain)
-    inc_high = lax.ppermute(edge_inc[:, :edge], "member", down)
-    inc_low = lax.ppermute(edge_inc[:, edge:], "member", up)
-    own_inc = increment(weights, own_gain)
+    cover_pad = jnp.pad(cover_all, ((spread, spread), (0, 0)))
+    covers = lax.dynamic_slice_in_dim(cover_pad, first, per_device + 2 * spread, axis=0)
+    split = half // PIECE_LENGTH
+    low_gain = masked_gain(low_states, perturbed, covers[:spread])
+    high_gain = masked_gain(high_states, perturbed, covers[per_device + spread :])
+    first_gain = masked_gain(first_states, perturbed, covers[spread : spread + split])
+    second_gain = masked_gain(
+        second_states, perturbed, covers[spread + split : spread + per_device]
+    )
+    inc_high = lax.ppermute(times_transposed(weights, low_gain), "member", down)
+    inc_low = lax.ppermute(times_transposed(weights, high_gain), "member", up)
+    first_inc = times_transposed(weights, first_gain)
+    second_inc = times_transposed(weights, second_gain)
     bounds = lax.dynamic_slice_in_dim(window_piece_offsets[0], patch, 2) - first
     block = jnp.arange(own_width) // PIECE_LENGTH
     from_low = (block < bounds[0])[None, :edge]
     from_high = (block >= bounds[1])[None, own_width - edge :]
-    result = states + jnp.concatenate(
+    tail = own_width - half - edge
+    centre = jnp.concatenate(
         [
-            jnp.where(from_low, inc_low, own_inc[:, :edge]),
-            own_inc[:, edge : own_width - edge],
-            jnp.where(from_high, inc_high, own_inc[:, own_width - edge :]),
+            first_states[:, edge:] + first_inc[:, edge:],
+            second_states[:, :tail] + second_inc[:, :tail],
         ],
         axis=1,
     )
-    returned = to_owners(result)
-    return (
-        returned.reshape(groups, rows, own_width).transpose(1, 0, 2).reshape(rows, variable_total)
-    )
+    centre_back = to_owners(centre)
+    sides = jnp.concatenate(
+        [
+            first_states[:, :edge] + jnp.where(from_low, inc_low, first_inc[:, :edge]),
+            second_states[:, tail:] + jnp.where(from_high, inc_high, second_inc[:, tail:]),
+        ],
+        axis=1,
+    )
+    sides_back = to_owners(sides)
+    return state_join(centre_back, sides_back, groups, row)
+
+
+def row_length(mesh):
+    devices = mesh.devices[:, 0].tolist()
+    count = len(devices)
+    spots = [getattr(d, "coords", None) for d in devices]
+    if any(spot is None for spot in spots):
+        return count
+    row = 1
+    while row < count and spots[row][2] == spots[0][2]:
+        row += 1
+    return row if count % row == 0 else count
 
 
 def solution(mesh):
     return jax.shard_map(
-        body,
+        functools.partial(body, row_length(mesh)),
         mesh=mesh,
         in_specs=(
             P("member", "region"),

time: 509 us -> 468 us (0.919)
  blocking collectives: 101 us -> 71.5 us
  waiting for transfers between devices: 147 us -> 128 us
  other arithmetic: 137 us -> 119 us
  starting transfers between devices: 25 us -> 41 us
  Pallas kernels: 11.4 us -> 24.6 us
  local copies, waits for them, and re-layouts: 34.9 us -> 26.9 us
  matrix products: 45.5 us -> 50.7 us
    ppermute x4, waiting for transfers between devices: 99.1 us -> 25.1 us  [the longest x1 20.2 us: body(): inc_low = lax.ppermute(times_transposed(weights, high_gain), 'member', up)]
    all_to_all x2 -> x5, waiting for transfers between devices: 34.3 us -> 93.1 us  [to_owners(): lax.all_to_all(rows_by_owner, 'member', split_axis=0, concat_axis=0, tile...]
    all_to_all x1, blocking collectives: 101 us -> 71.5 us  [to_owners(): lax.all_to_all(rows_by_owner, 'member', split_axis=0, concat_axis=0, tile...]
    another operation x17 -> x20, other arithmetic: 120 us -> 99.3 us  [the longest x12 53.2 us: factor_block(): lower = jnp.linalg.cholesky(block)]
    dot_general x2 -> x24, matrix products: 12.1 us -> 30.2 us  [the longest x17 21.9 us: times_transposed(): lax.dot_general(left, right, (((1,), (1,)), ((), ())), precision=precisio...]
    another operation x20 -> x4, matrix products: 19.8 us -> 2.6 us  [factor_block(): lax.linalg.triangular_solve(lower, jnp.eye(PIECE_LENGTH, dtype=jnp.float3...]
    all_to_all x2 -> x5, starting transfers between devices: 10.6 us -> 26.3 us  [to_owners(): lax.all_to_all(rows_by_owner, 'member', split_axis=0, concat_axis=0, tile...]
    another operation x17 -> x1, local copies, waits for them, and re-layouts: 14.2 us -> 0.61 us  [body(): sorted_lists = jnp.stack([lists[snake(i, row)] for i in range(groups)])]
  transfers between devices with their start and end apart: 10 -> 13, of which waited for: 6 -> 8; matrix products, arithmetic and copies ran while one was open for 38% -> 36% of each run, Pallas kernels for 1% -> 2%
where the time goes in v2:
time: 468 us; the launch traced here: 463 us
  waiting for transfers between devices  128 us (27%)
  other arithmetic  119 us (25%)
  blocking collectives  71.5 us (15%)
  matrix products  50.7 us (11%)
  starting transfers between devices  41 us (9%)
  local copies, waits for them, and re-layouts  26.9 us (6%)
  Pallas kernels  24.6 us (5%)
    all_to_all x5, waiting for transfers between devices, to_owners(): lax.all_to_all(rows_by_owner, 'member', split_axis=0, concat_axis=0, tile...  93.1 us
    all_to_all x1, blocking collectives, to_owners(): lax.all_to_all(rows_by_owner, 'member', split_axis=0, concat_axis=0, tile...  71.5 us
    another operation x12, other arithmetic, factor_block(): lower = jnp.linalg.cholesky(block)  53.2 us
    another operation x8, other arithmetic, factor_block(): lax.linalg.triangular_solve(lower, jnp.eye(PIECE_LENGTH, dtype=jnp.float3...  46.1 us
    all_to_all x5, starting transfers between devices, to_owners(): lax.all_to_all(rows_by_owner, 'member', split_axis=0, concat_axis=0, tile...  26.3 us
    dot_general x17, matrix products, times_transposed(): lax.dot_general(left, right, (((1,), (1,)), ((), ())), precision=precisio...  21.9 us
    ppermute x1, waiting for transfers between devices, body(): inc_low = lax.ppermute(times_transposed(weights, high_gain), 'member', up)  20.2 us
    dot_general x4, matrix products, masked_gain(): lax.dot_general(centred, perturbed, (((0,), (0,)), ((), ())), precision=h...  14.3 us
  transfers between devices with their start and end apart: 13, of which 8 were waited for; matrix products, arithmetic and copies ran while one was open for 36% of the time, Pallas kernels for 2%

profile of v2, /device:TPU:0, one launch (start us, length us, event | category | flops | bytes accessed | tf_op | source)
XLA Modules:
  0.0 463.5 jit_solution(10817803269905648572)
XLA Ops:
  0.0 6.6 %state_pack.1 = (f32[1024,512]{1,0:T(8,128)}, f32[1024,512]{1,0:T(8,128)}) custom-call(f32[128,8192]{1,0:T(8,128)} %in_ref.1), custom_call_target="tpu_custom_call" | custom-call | tf_op jit(solution)/shard_map/state_pack/pallas_call | solution.py:109
  6.6 7.4 %all-to-all-start = ((f32[8,128,512]{2,1,0:T(8,128)}), f32[8,128,512]{2,1,0:T(8,128)S(1)}, u32[]{:S(2)}, u32[]{:S(2)}) async-start(f32[8,128,512]{2,1,0:T(8,128)} %bitcast.150), calls=%async_computation | async-start | bytes 4194304 | tf_op jit(solution)/shard_map/all_to_all | solution.py:93
  17.1 3.4 halo_pack.1
  23.9 9.3 %collective-permute-done.before_ref = f32[128,1024]{1,0:T(8,128)S(1)} collective-permute-done((f32[128,1024]{1,0:T(8,128)}, f32[128,1024]{1,0:T(8,128)S(1)}, u32[]{:S(2)}, u32[]{:S(2)}) %collective-permute-start) | collective-permute-done | bytes 524320 | tf_op jit(solution)/shard_map/ppermute | solution.py:21
  34.8 4.0 window_pack.3
  38.8 4.0 window_pack.2
  42.8 19.4 %all-to-all-done = f32[8,128,512]{2,1,0:T(8,128)S(1)} async-done(((f32[8,128,512]{2,1,0:T(8,128)}), f32[8,128,512]{2,1,0:T(8,128)S(1)}, u32[]{:S(2)}, u32[]{:S(2)}) %all-to-all-start) | async-done | bytes 2097184 | tf_op jit(solution)/shard_map/all_to_all | solution.py:93
  62.3 1.9 copy.31
  64.1 3.8 all-to-all-start.1
  68.5 47.8 %all-to-all-done.1 = f32[8,128,512]{2,1,0:T(8,128)S(1)} async-done(((f32[8,128,512]{2,1,0:T(8,128)}), f32[8,128,512]{2,1,0:T(8,128)S(1)}, u32[]{:S(2)}, u32[]{:S(2)}) %all-to-all-start.1) | async-done | bytes 2097184 | tf_op jit(solution)/shard_map/all_to_all | solution.py:93
  116.3 2.7 slice.198
  122.3 6.2 %all-to-all-start.2 = ((f32[8,128,512]{2,1,0:T(8,128)}), f32[8,128,512]{2,1,0:T(8,128)}, u32[]{:S(2)}, u32[]{:S(2)}) async-start(f32[8,128,512]{2,1,0:T(8,128)} %bitcast.149), calls=%async_computation.2 | async-start | bytes 4194304 | tf_op jit(solution)/shard_map/all_to_all | solution.py:93
  128.6 3.6 fusion.35
  132.3 11.7 %cholesky.74 = f32[128,128]{1,0:T(8,128)S(1)} custom-call(f32[128,128]{1,0:T(8,128)S(1)} %fusion.112), custom_call_target="Cholesky" | custom-call | tf_op jit(solution)/shard_map/jit(cholesky)/cholesky | solution.py:174
  145.2 9.8 %custom-call.8 = f32[1,128,128]{1,2,0:T(8,128)S(1)} custom-call(f32[1,128,128]{2,1,0:T(8,128)S(1)} %fusion.101), custom_call_target="InvertDiagBlocksLowerTriangular" | custom-call | tf_op jit(solution)/shard_map/triangular_solve/custom-call.0 | solution.py:175
  158.3 12.2 %cholesky.85 = f32[128,128]{1,0:T(8,128)S(1)} custom-call(f32[128,128]{1,0:T(8,128)S(1)} %fusion.110), custom_call_target="Cholesky" | custom-call | tf_op jit(solution)/shard_map/jit(cholesky)/cholesky | solution.py:174
  171.7 9.8 %custom-call.9 = f32[1,128,128]{1,2,0:T(8,128)S(1)} custom-call(f32[1,128,128]{2,1,0:T(8,128)S(1)} %fusion.102), custom_call_target="InvertDiagBlocksLowerTriangular" | custom-call | tf_op jit(solution)/shard_map/triangular_solve/custom-call.0 | solution.py:175
  183.9 2.1 fusion.43
  187.6 13.9 %all-to-all-done.2 = f32[8,128,512]{2,1,0:T(8,128)} async-done(((f32[8,128,512]{2,1,0:T(8,128)}), f32[8,128,512]{2,1,0:T(8,128)}, u32[]{:S(2)}, u32[]{:S(2)}) %all-to-all-start.2) | async-done | bytes 2097184 | tf_op jit(solution)/shard_map/all_to_all | solution.py:93
  201.5 2.9 copy.32
  204.4 4.3 all-to-all-start.3
  208.8 3.8 fusion.53
  216.5 12.5 %cholesky.96 = f32[128,128]{1,0:T(8,128)S(1)} custom-call(f32[128,128]{1,0:T(8,128)} %fusion.108), custom_call_target="Cholesky" | custom-call | tf_op jit(solution)/shard_map/jit(cholesky)/cholesky | solution.py:174
  231.1 10.6 %custom-call.10 = f32[1,128,128]{1,2,0:T(8,128)S(1)} custom-call(f32[1,128,128]{2,1,0:T(8,128)} %fusion.103), custom_call_target="InvertDiagBlocksLowerTriangular" | custom-call | tf_op jit(solution)/shard_map/triangular_solve/custom-call.0 | solution.py:175
  241.8 2.9 slice.203
  244.6 5.1 %collective-permute-start.6 = (f32[1024,384]{0,1:T(8,128)}, f32[1024,384]{0,1:T(8,128)}, u32[]{:S(2)}, u32[]{:S(2)}) collective-permute-start(f32[1024,384]{0,1:T(8,128)} %slice.203), channel_id=1, source_target_pairs={{0,4},{4,12},{12,8},{8,16},{16,20},{20,28},{28,24},{1,5},{5,13},{1... | collective-permute-start | bytes 4718600 | tf_op jit(solution)/shard_map/ppermute | solution.py:277
  251.8 2.4 reduce_sum.47
  257.2 13.2 %cholesky.107 = f32[128,128]{1,0:T(8,128)} custom-call(f32[128,128]{1,0:T(8,128)} %fusion.106), custom_call_target="Cholesky" | custom-call | tf_op jit(solution)/shard_map/jit(cholesky)/cholesky | solution.py:174
  271.9 2.1 fusion.104
  274.0 11.3 %custom-call.11 = f32[1,128,128]{1,2,0:T(8,128)} custom-call(f32[1,128,128]{2,1,0:T(8,128)} %fusion.104), custom_call_target="InvertDiagBlocksLowerTriangular" | custom-call | tf_op jit(solution)/shard_map/triangular_solve/custom-call.0 | solution.py:175
  288.4 4.6 fusion.38
  294.6 3.9 fusion.63
  300.2 3.1 slice_subtract_fusion
  311.4 2.7 fusion.68
  315.0 2.7 fusion.131
  317.7 3.6 collective-permute-start.5
  321.3 1.9 fusion.133
  323.2 2.7 fusion.130
  327.3 1.9 fusion.132
  333.1 4.5 all-to-all-start.4
  339.6 20.2 %collective-permute-done.5 = f32[1024,384]{0,1:T(8,128)} collective-permute-done((f32[1024,384]{0,1:T(8,128)}, f32[1024,384]{0,1:T(8,128)}, u32[]{:S(2)}, u32[]{:S(2)}) %collective-permute-start.5) | collective-permute-done | bytes 1572896 | tf_op jit(solution)/shard_map/ppermute | solution.py:301
  359.8 2.2 fusion.13
  362.0 5.0 %collective-permute-done.7 = f32[1024,384]{0,1:T(8,128)} collective-permute-done((f32[1024,384]{0,1:T(8,128)}, f32[1024,384]{0,1:T(8,128)}, u32[]{:S(2)}, u32[]{:S(2)}) %collective-permute-start.7) | collective-permute-done | bytes 1572896 | tf_op jit(solution)/shard_map/ppermute | solution.py:300
  368.7 1.9 pad_maximum_fusion
  370.6 2.4 copy.34
  373.0 11.9 %all-to-all-done.4 = f32[8,128,256]{2,1,0:T(8,128)} async-done(((f32[8,128,256]{2,1,0:T(8,128)}), f32[8,128,256]{2,1,0:T(8,128)}, u32[]{:S(2)}, u32[]{:S(2)}) %all-to-all-start.4) | async-done | bytes 1048608 | tf_op jit(solution)/shard_map/all_to_all | solution.py:93
  384.9 71.5 %all_to_all.70 = f32[8,128,768]{2,1,0:T(8,128)} all-to-all(f32[8,128,768]{2,1,0:T(8,128)S(1)} %bitcast.140), channel_id=1, replica_groups=mesh['member'=8,'region'=4] {'member'}, dimensions={0} | all-to-all | bytes 6291456 | tf_op jit(solution)/shard_map/all_to_all | solution.py:93
  456.4 6.6 %state_join.1 = f32[128,8192]{1,0:T(8,128)} custom-call(f32[1024,256]{1,0:T(8,128)} %bitcast.30.centre_ref, f32[1024,768]{1,0:T(8,128)} %bitcast.141), custom_call_target="tpu_custom_call" | custom-call | tf_op jit(solution)/shard_map/state_join/pallas_call | solution.py:136
  (156 shorter events, 58.5 us)
Async XLA Ops:
  6.6 7.4 %copy-start.22 = (s32[1,2,4]{2,1,0:T(2,128)S(1)}, s32[1,2,4]{2,1,0:T(2,128)}, u32[]{:S(2)}) copy-start(s32[1,2,4]{2,1,0:T(2,128)} %param.19) | copy-start | bytes 100
  6.6 7.5 %copy-start.21 = (f32[4096]{0:T(1024)S(1)}, f32[4096]{0:T(1024)}, u32[]{:S(2)}) copy-start(f32[4096]{0:T(1024)} %param.16) | copy-start | bytes 49156
  6.6 55.7 %all-to-all-start = ((f32[8,128,512]{2,1,0:T(8,128)}), f32[8,128,512]{2,1,0:T(8,128)S(1)}, u32[]{:S(2)}, u32[]{:S(2)}) async-start(f32[8,128,512]{2,1,0:T(8,128)} %bitcast.150), calls=%async_computation | async-start | bytes 4194304 | tf_op jit(solution)/shard_map/all_to_all | solution.py:93
  14.7 8.5 %collective-permute-start.2 = (f32[4,128]{1,0:T(4,128)S(1)}, f32[4,128]{1,0:T(4,128)S(1)}, u32[]{:S(2)}, u32[]{:S(2)}) collective-permute-start(f32[4,128]{1,0:T(4,128)S(1)} %broadcast_select_fusion.1), channel_id=1, source_target_pairs={{0,1},{1,2},{2,3},{3,0},{4,5},{5,6},{6,7},{7,4},{8,9},{9,10},{10,1... | collective-permute-start | bytes 6152 | tf_op jit(solution)/shard_map/ppermute | solution.py:21
  15.4 7.8 %collective-permute-start.3 = (f32[4,128]{1,0:T(4,128)S(1)}, f32[4,128]{1,0:T(4,128)S(1)}, u32[]{:S(2)}, u32[]{:S(2)}) collective-permute-start(f32[4,128]{1,0:T(4,128)S(1)} %broadcast_select_fusion), channel_id=1, source_target_pairs={{0,3},{1,0},{2,1},{3,2},{4,7},{5,4},{6,5},{7,6},{8,11},{9,8},{10,9... | collective-permute-start | bytes 6152 | tf_op jit(solution)/shard_map/ppermute | solution.py:21
  17.1 5.1 %copy-start.20 = (s32[1,8,4]{1,2,0:T(4,128)S(1)}, s32[1,8,4]{1,2,0:T(4,128)}, u32[]{:S(2)}) copy-start(s32[1,8,4]{1,2,0:T(4,128)} %param.18) | copy-start | bytes 388
  20.5 12.7 %collective-permute-start = (f32[128,1024]{1,0:T(8,128)}, f32[128,1024]{1,0:T(8,128)S(1)}, u32[]{:S(2)}, u32[]{:S(2)}) collective-permute-start(f32[128,1024]{1,0:T(8,128)} %get-tuple-element.25), channel_id=1, source_target_pairs={{0,1},{1,2},{2,3},{3,0},{4,5},{5,6},{6,7},{7,4},{8,9},{9,10},{10,1... | collective-permute-start | bytes 1572872 | tf_op jit(solution)/shard_map/ppermute | solution.py:21
  20.5 13.5 %collective-permute-start.1 = (f32[128,1024]{1,0:T(8,128)}, f32[128,1024]{1,0:T(8,128)S(1)}, u32[]{:S(2)}, u32[]{:S(2)}) collective-permute-start(f32[128,1024]{1,0:T(8,128)} %get-tuple-element.26), channel_id=1, source_target_pairs={{0,3},{1,0},{2,1},{3,2},{4,7},{5,4},{6,5},{7,6},{8,11},{9,8},{10,9... | collective-permute-start | bytes 1572872 | tf_op jit(solution)/shard_map/ppermute | solution.py:21
  33.1 0.9 copy-start.7
  34.0 0.8 copy-start.8
  64.1 3.8 copy-start.23
  64.1 52.2 %all-to-all-start.1 = ((f32[8,128,512]{2,1,0:T(8,128)}), f32[8,128,512]{2,1,0:T(8,128)S(1)}, u32[]{:S(2)}, u32[]{:S(2)}) async-start(f32[8,128,512]{2,1,0:T(8,128)} %bitcast.144), calls=%async_computation.1 | async-start | bytes 4194304 | tf_op jit(solution)/shard_map/all_to_all | solution.py:93
  119.1 66.9 %collective-permute-start.4 = (f32[1024,384]{0,1:T(8,128)}, f32[1024,384]{0,1:T(8,128)}, u32[]{:S(2)}, u32[]{:S(2)}) collective-permute-start(f32[1024,384]{0,1:T(8,128)} %slice.198), channel_id=1, source_target_pairs={{4,0},{12,4},{8,12},{16,8},{20,16},{28,20},{24,28},{5,1},{13,5},{9... | collective-permute-start | bytes 4718600 | tf_op jit(solution)/shard_map/ppermute | solution.py:262
  122.3 79.2 %all-to-all-start.2 = ((f32[8,128,512]{2,1,0:T(8,128)}), f32[8,128,512]{2,1,0:T(8,128)}, u32[]{:S(2)}, u32[]{:S(2)}) async-start(f32[8,128,512]{2,1,0:T(8,128)} %bitcast.149), calls=%async_computation.2 | async-start | bytes 4194304 | tf_op jit(solution)/shard_map/all_to_all | solution.py:93
  132.2 23.2 %copy-start.16 = (f32[512,512]{0,1:T(8,128)}, f32[512,512]{0,1:T(8,128)S(1)}, u32[]{:S(2)}) copy-start(f32[512,512]{0,1:T(8,128)S(1)} %fusion.35) | copy-start | bytes 3145732
  155.3 0.6 copy-start.9
  181.5 2.4 copy-start
  181.8 2.1 copy-start.11
  204.4 94.1 %all-to-all-start.3 = ((f32[8,128,512]{2,1,0:T(8,128)}), f32[8,128,512]{2,1,0:T(8,128)}, u32[]{:S(2)}, u32[]{:S(2)}) async-start(f32[8,128,512]{2,1,0:T(8,128)} %bitcast.142), calls=%async_computation.3 | async-start | bytes 4194304 | tf_op jit(solution)/shard_map/all_to_all | solution.py:93
  241.8 8.9 %copy-start.15 = (f32[256,256]{0,1:T(8,128)S(1)}, f32[256,256]{0,1:T(8,128)}, u32[]{:S(2)}) copy-start(f32[256,256]{0,1:T(8,128)} %convolution_subtract_fusion.5) | copy-start | bytes 786436
  244.6 48.3 %collective-permute-start.6 = (f32[1024,384]{0,1:T(8,128)}, f32[1024,384]{0,1:T(8,128)}, u32[]{:S(2)}, u32[]{:S(2)}) collective-permute-start(f32[1024,384]{0,1:T(8,128)} %slice.203), channel_id=1, source_target_pairs={{0,4},{4,12},{12,8},{8,16},{16,20},{20,28},{28,24},{1,5},{5,13},{1... | collective-permute-start | bytes 4718600 | tf_op jit(solution)/shard_map/ppermute | solution.py:277
  250.0 0.6 copy-start.13
  300.1 3.1 copy-start.12
  303.2 1.6 copy-start.14
  303.8 2.2 copy-start.19
  310.7 3.4 copy-start.10
  311.4 3.6 copy-start.17
  317.7 5.5 %copy-start.18 = (f32[384,512]{1,0:T(8,128)S(1)}, f32[384,512]{1,0:T(8,128)}, u32[]{:S(2)}) copy-start(f32[384,512]{1,0:T(8,128)} %fusion.63) | copy-start | bytes 2359300
  317.7 42.1 %collective-permute-start.5 = (f32[1024,384]{0,1:T(8,128)}, f32[1024,384]{0,1:T(8,128)}, u32[]{:S(2)}, u32[]{:S(2)}) collective-permute-start(f32[1024,384]{0,1:T(8,128)} %fusion.131), channel_id=1, source_target_pairs={{0,4},{4,12},{12,8},{8,16},{16,20},{20,28},{28,24},{1,5},{5,13},{1... | collective-permute-start | bytes 4718600 | tf_op jit(solution)/shard_map/ppermute | solution.py:301
  323.2 4.0 copy-start.3
  323.2 4.0 copy-start.1
  323.2 4.1 copy-start.6
  325.9 41.0 %collective-permute-start.7 = (f32[1024,384]{0,1:T(8,128)}, f32[1024,384]{0,1:T(8,128)}, u32[]{:S(2)}, u32[]{:S(2)}) collective-permute-start(f32[1024,384]{0,1:T(8,128)} %fusion.130), channel_id=1, source_target_pairs={{4,0},{12,4},{8,12},{16,8},{20,16},{28,20},{24,28},{5,1},{13,5},{9... | collective-permute-start | bytes 4718600 | tf_op jit(solution)/shard_map/ppermute | solution.py:300
  329.2 1.4 copy-start.4
  331.7 5.8 %copy-start.24 = (s32[1,9]{1,0:T(1,128)S(1)}, s32[1,9]{1,0:T(1,128)}, u32[]{:S(2)}) copy-start(s32[1,9]{1,0:T(1,128)} %param.17) | copy-start | bytes 112
  333.1 51.8 %all-to-all-start.4 = ((f32[8,128,256]{2,1,0:T(8,128)}), f32[8,128,256]{2,1,0:T(8,128)}, u32[]{:S(2)}, u32[]{:S(2)}) async-start(f32[8,128,256]{2,1,0:T(8,128)} %bitcast.29), calls=%async_computation.4 | async-start | bytes 2097152 | tf_op jit(solution)/shard_map/all_to_all | solution.py:93
  339.6 27.3 %copy-start.2 = (f32[1024,512]{0,1:T(8,128)S(1)}, f32[1024,512]{0,1:T(8,128)}, u32[]{:S(2)}) copy-start(f32[1024,512]{0,1:T(8,128)} %copy.32) | copy-start | bytes 6291460
  339.6 27.3 %copy-start.5 = (f32[1024,512]{0,1:T(8,128)S(1)}, f32[1024,512]{0,1:T(8,128)}, u32[]{:S(2)}) copy-start(f32[1024,512]{0,1:T(8,128)} %copy-done.4) | copy-start | bytes 6291460

commit v3 on v2

--- a/solution.py
+++ b/solution.py
@@ -170,11 +170,47 @@
     )
 
 
+def factor_kernel(block_ref, inverse_ref, work_ref):
+    size = block_ref.shape[0]
+    wide = 2 * size
+    eye = lax.broadcasted_iota(jnp.int32, (size, size), 0) == lax.broadcasted_iota(
+        jnp.int32, (size, size), 1
+    )
+    work_ref[:, :size] = block_ref[...]
+    work_ref[:, size:] = eye.astype(jnp.float32)
+    step_rows = 8
+    row_ids = lax.broadcasted_iota(jnp.int32, (step_rows, wide), 0)
+    for start in range(0, size, step_rows):
+        rows = work_ref[start : start + step_rows, :]
+        for j in range(step_rows):
+            column = rows[:, start + j : start + j + 1]
+            scale = 1.0 / jnp.sqrt(column[j : j + 1, :])
+            pivot = rows[j : j + 1, :] * scale
+            lowered = rows - (column * scale) * pivot
+            rows = jnp.where(row_ids > j, lowered, jnp.where(row_ids == j, pivot, rows))
+        inverse_ref[start : start + step_rows, :] = rows[:, size:]
+        after = start + step_rows
+        if after < size:
+            change = lax.dot_general(
+                rows[:, :size],
+                rows,
+                (((0,), (0,)), ((), ())),
+                precision=highest,
+                preferred_element_type=jnp.float32,
+            )
+            work_ref[after:, :] = work_ref[after:, :] - change[after:, :]
+
+
 def factor_block(block):
-    lower = jnp.linalg.cholesky(block)
-    return lax.linalg.triangular_solve(
-        lower, jnp.eye(PIECE_LENGTH, dtype=jnp.float32), left_side=True, lower=True
-    )
+    size = block.shape[0]
+    return pl.pallas_call(
+        factor_kernel,
+        out_shape=jax.ShapeDtypeStruct((size, size), jnp.float32),
+        in_specs=[pl.BlockSpec(memory_space=pltpu.VMEM)],
+        out_specs=pl.BlockSpec(memory_space=pltpu.VMEM),
+        scratch_shapes=[pltpu.VMEM((size, 2 * size), jnp.float32)],
+        name="factor_block",
+    )(block)
 
 
 def factor_step(trailing):

time: 468 us -> 452 us (0.966)
  other arithmetic: 119 us -> 15.7 us
  Pallas kernels: 24.6 us -> 96.8 us
  waiting for transfers between devices: 128 us -> 61.8 us
  blocking collectives: 71.5 us -> 121 us
  starting transfers between devices: 41 us -> 73.2 us
    another operation x20 -> x0, other arithmetic: 99.3 us -> none  [the longest x12 53.2 us: factor_block(): lower = jnp.linalg.cholesky(block)]
    pallas_call x0 -> x4, Pallas kernels: none -> 72.2 us  [factor_block(): pl.pallas_call(factor_kernel, out_shape=jax.ShapeDtypeStruct((size, size)...]
    all_to_all x5 -> x4, waiting for transfers between devices: 93.1 us -> 30.2 us  [to_owners(): lax.all_to_all(rows_by_owner, 'member', split_axis=0, concat_axis=0, tile...]
    all_to_all x1 -> x2, blocking collectives: 71.5 us -> 121 us  [to_owners(): lax.all_to_all(rows_by_owner, 'member', split_axis=0, concat_axis=0, tile...]
    all_to_all x5 -> x4, starting transfers between devices: 26.3 us -> 54.5 us  [to_owners(): lax.all_to_all(rows_by_owner, 'member', split_axis=0, concat_axis=0, tile...]
    ppermute x1, waiting for transfers between devices: 20.2 us -> 0.01 us  [body(): inc_low = lax.ppermute(times_transposed(weights, high_gain), 'member', up)]
    ppermute x1, waiting for transfers between devices: 4.97 us -> 23.8 us  [body(): inc_high = lax.ppermute(times_transposed(weights, low_gain), 'member', down)]
    ppermute x1, starting transfers between devices: 5.09 us -> 9.82 us  [body(): lax.ppermute(second_states[:, own_width - half - edge:], 'member', up)]
  transfers between devices with their start and end apart: 13 -> 12, of which waited for: 8 -> 5; matrix products, arithmetic and copies ran while one was open for 36% -> 16% of each run, Pallas kernels for 2% -> 19%
where the time goes in v3:
time: 452 us; the launch traced here: 447 us
  blocking collectives  121 us (27%)
  Pallas kernels  96.8 us (21%)
  starting transfers between devices  73.2 us (16%)
  waiting for transfers between devices  61.8 us (14%)
  matrix products  52.3 us (12%)
  local copies, waits for them, and re-layouts  25.5 us (6%)
  other arithmetic  15.7 us (3%)
    all_to_all x2, blocking collectives, to_owners(): lax.all_to_all(rows_by_owner, 'member', split_axis=0, concat_axis=0, tile...  121 us
    pallas_call x4, Pallas kernels, factor_block(): pl.pallas_call(factor_kernel, out_shape=jax.ShapeDtypeStruct((size, size)...  72.2 us
    all_to_all x4, starting transfers between devices, to_owners(): lax.all_to_all(rows_by_owner, 'member', split_axis=0, concat_axis=0, tile...  54.5 us
    all_to_all x4, waiting for transfers between devices, to_owners(): lax.all_to_all(rows_by_owner, 'member', split_axis=0, concat_axis=0, tile...  30.2 us
    dot_general x17, matrix products, times_transposed(): lax.dot_general(left, right, (((1,), (1,)), ((), ())), precision=precisio...  24.8 us
    ppermute x1, waiting for transfers between devices, body(): inc_high = lax.ppermute(times_transposed(weights, low_gain), 'member', down)  23.8 us
    dot_general x4, matrix products, masked_gain(): lax.dot_general(centred, perturbed, (((0,), (0,)), ((), ())), precision=h...  15.7 us
    ppermute x1, starting transfers between devices, body(): lax.ppermute(second_states[:, own_width - half - edge:], 'member', up)  9.82 us
  transfers between devices with their start and end apart: 12, of which 5 were waited for; matrix products, arithmetic and copies ran while one was open for 16% of the time, Pallas kernels for 19%

profile of v3, /device:TPU:0, one launch (start us, length us, event | category | flops | bytes accessed | tf_op | source)
XLA Modules:
  0.0 447.3 jit_solution(8898684186288799154)
XLA Ops:
  0.0 6.6 %state_pack.1 = (f32[1024,512]{1,0:T(8,128)}, f32[1024,512]{1,0:T(8,128)}) custom-call(f32[128,8192]{1,0:T(8,128)} %in_ref.1), custom_call_target="tpu_custom_call" | custom-call | tf_op jit(solution)/shard_map/state_pack/pallas_call | solution.py:109
  6.6 7.3 %all-to-all-start = ((f32[8,128,512]{2,1,0:T(8,128)}), f32[8,128,512]{2,1,0:T(8,128)S(1)}, u32[]{:S(2)}, u32[]{:S(2)}) async-start(f32[8,128,512]{2,1,0:T(8,128)} %bitcast.114), calls=%async_computation | async-start | bytes 4194304 | tf_op jit(solution)/shard_map/all_to_all | solution.py:93
  13.9 3.4 halo_pack.1
  17.3 1.7 collective-permute-start.1
  20.4 1.7 collective-permute-start.3
  23.1 6.9 %collective-permute-done.2 = f32[4,128]{1,0:T(4,128)S(1)} collective-permute-done((f32[4,128]{1,0:T(4,128)S(1)}, f32[4,128]{1,0:T(4,128)S(1)}, u32[]{:S(2)}, u32[]{:S(2)}) %collective-permute-start.2) | collective-permute-done | bytes 2080 | tf_op jit(solution)/shard_map/ppermute | solution.py:21
  33.1 4.0 window_pack.2
  37.1 4.0 window_pack.3
  41.1 21.0 %all-to-all-done = f32[8,128,512]{2,1,0:T(8,128)S(1)} async-done(((f32[8,128,512]{2,1,0:T(8,128)}), f32[8,128,512]{2,1,0:T(8,128)S(1)}, u32[]{:S(2)}, u32[]{:S(2)}) %all-to-all-start) | async-done | bytes 2097184 | tf_op jit(solution)/shard_map/all_to_all | solution.py:93
  62.2 1.9 copy.21
  64.0 52.0 %all_to_all.70 = f32[8,128,512]{2,1,0:T(8,128)S(1)} all-to-all(f32[8,128,512]{2,1,0:T(8,128)} %bitcast.108), channel_id=1, replica_groups=mesh['member'=8,'region'=4] {'member'}, dimensions={0} | all-to-all | bytes 4194304 | tf_op jit(solution)/shard_map/all_to_all | solution.py:93
  116.0 4.5 %all-to-all-start.2 = ((f32[8,128,512]{2,1,0:T(8,128)}), f32[8,128,512]{2,1,0:T(8,128)}, u32[]{:S(2)}, u32[]{:S(2)}) async-start(f32[8,128,512]{2,1,0:T(8,128)} %bitcast.113), calls=%async_computation.2 | async-start | bytes 4194304 | tf_op jit(solution)/shard_map/all_to_all | solution.py:93
  120.8 2.7 slice.192
  125.0 1.8 reduce_sum.46
  127.0 3.6 fusion.35
  131.3 17.9 %factor_block.4 = f32[128,128]{1,0:T(8,128)} custom-call(f32[128,128]{1,0:T(8,128)} %slice.210.block_ref), custom_call_target="tpu_custom_call" | custom-call | tf_op jit(solution)/shard_map/factor_block/pallas_call | solution.py:206
  150.4 1.7 convolution_subtract_fusion.1
  152.7 18.3 %factor_block.5 = f32[128,128]{1,0:T(8,128)} custom-call(f32[128,128]{1,0:T(8,128)} %slice.213.block_ref), custom_call_target="tpu_custom_call" | custom-call | tf_op jit(solution)/shard_map/factor_block/pallas_call | solution.py:206
  173.3 2.9 copy.22
  176.1 8.3 %all-to-all-start.3 = ((f32[8,128,512]{2,1,0:T(8,128)}), f32[8,128,512]{2,1,0:T(8,128)}, u32[]{:S(2)}, u32[]{:S(2)}) async-start(f32[8,128,512]{2,1,0:T(8,128)} %bitcast.107), calls=%async_computation.3 | async-start | bytes 4194304 | tf_op jit(solution)/shard_map/all_to_all | solution.py:93
  185.8 3.5 fusion.43
  190.9 2.7 slice.197
  193.6 9.8 %collective-permute-start.6 = (f32[1024,384]{0,1:T(8,128)}, f32[1024,384]{0,1:T(8,128)}, u32[]{:S(2)}, u32[]{:S(2)}) collective-permute-start(f32[1024,384]{0,1:T(8,128)} %slice.197), channel_id=1, source_target_pairs={{0,4},{4,12},{12,8},{8,16},{16,20},{20,28},{28,24},{1,5},{5,13},{1... | collective-permute-start | bytes 4718600 | tf_op jit(solution)/shard_map/ppermute | solution.py:313
  203.5 3.8 fusion.53
  207.4 1.8 reduce_sum.47
  210.6 17.9 %factor_block.6 = f32[128,128]{1,0:T(8,128)} custom-call(f32[128,128]{1,0:T(8,128)} %slice.180.block_ref), custom_call_target="tpu_custom_call" | custom-call | tf_op jit(solution)/shard_map/factor_block/pallas_call | solution.py:206
  229.7 1.7 convolution_subtract_fusion.6.block_ref
  231.4 18.0 %factor_block.7 = f32[128,128]{1,0:T(8,128)} custom-call(f32[128,128]{1,0:T(8,128)} %convolution_subtract_fusion.6.block_ref), custom_call_target="tpu_custom_call" | custom-call | tf_op jit(solution)/shard_map/factor_block/pallas_call | solution.py:206
  250.2 4.4 fusion.38
  256.3 4.0 fusion.63
  260.3 1.6 fusion.87
  262.0 2.8 slice_subtract_fusion
  270.5 1.8 convolution_subtract_fusion.2
  273.0 3.0 fusion.68
  276.6 2.7 fusion.105
  279.2 2.7 collective-permute-start.5
  281.9 1.9 fusion.107
  283.8 2.7 fusion.104
  287.8 1.9 fusion.106
  293.6 34.4 %all-to-all-start.4 = ((f32[8,128,256]{2,1,0:T(8,128)}), f32[8,128,256]{2,1,0:T(8,128)}, u32[]{:S(2)}, u32[]{:S(2)}) async-start(f32[8,128,256]{2,1,0:T(8,128)} %bitcast.17), calls=%async_computation.4 | async-start | bytes 2097152 | tf_op jit(solution)/shard_map/all_to_all | solution.py:93
  330.1 2.3 fusion.13
  332.4 23.8 %collective-permute-done.7 = f32[1024,384]{0,1:T(8,128)} collective-permute-done((f32[1024,384]{0,1:T(8,128)}, f32[1024,384]{0,1:T(8,128)}, u32[]{:S(2)}, u32[]{:S(2)}) %collective-permute-start.7) | collective-permute-done | bytes 1572896 | tf_op jit(solution)/shard_map/ppermute | solution.py:336
  356.2 1.7 fusion.12
  357.9 1.9 pad_maximum_fusion
  359.8 2.4 copy.24
  362.2 9.2 %all-to-all-done.4 = f32[8,128,256]{2,1,0:T(8,128)} async-done(((f32[8,128,256]{2,1,0:T(8,128)}), f32[8,128,256]{2,1,0:T(8,128)}, u32[]{:S(2)}, u32[]{:S(2)}) %all-to-all-start.4) | async-done | bytes 1048608 | tf_op jit(solution)/shard_map/all_to_all | solution.py:93
  371.3 69.1 %all_to_all.71 = f32[8,128,768]{2,1,0:T(8,128)} all-to-all(f32[8,128,768]{2,1,0:T(8,128)S(1)} %bitcast.104), channel_id=1, replica_groups=mesh['member'=8,'region'=4] {'member'}, dimensions={0} | all-to-all | bytes 6291456 | tf_op jit(solution)/shard_map/all_to_all | solution.py:93
  440.4 6.6 %state_join.1 = f32[128,8192]{1,0:T(8,128)} custom-call(f32[1024,256]{1,0:T(8,128)} %bitcast.18.centre_ref, f32[1024,768]{1,0:T(8,128)} %bitcast.105), custom_call_target="tpu_custom_call" | custom-call | tf_op jit(solution)/shard_map/state_join/pallas_call | solution.py:136
  (121 shorter events, 34.1 us)
Async XLA Ops:
  6.6 55.5 %all-to-all-start = ((f32[8,128,512]{2,1,0:T(8,128)}), f32[8,128,512]{2,1,0:T(8,128)S(1)}, u32[]{:S(2)}, u32[]{:S(2)}) async-start(f32[8,128,512]{2,1,0:T(8,128)} %bitcast.114), calls=%async_computation | async-start | bytes 4194304 | tf_op jit(solution)/shard_map/all_to_all | solution.py:93
  13.9 5.1 %copy-start.17 = (s32[1,2,4]{2,1,0:T(2,128)S(1)}, s32[1,2,4]{2,1,0:T(2,128)}, u32[]{:S(2)}) copy-start(s32[1,2,4]{2,1,0:T(2,128)} %param.16) | copy-start | bytes 100
  13.9 5.2 %copy-start.16 = (f32[4096]{0:T(1024)S(1)}, f32[4096]{0:T(1024)}, u32[]{:S(2)}) copy-start(f32[4096]{0:T(1024)} %param.13) | copy-start | bytes 49156
  13.9 8.2 %copy-start.15 = (s32[1,8,4]{1,2,0:T(4,128)S(1)}, s32[1,8,4]{1,2,0:T(4,128)}, u32[]{:S(2)}) copy-start(s32[1,8,4]{1,2,0:T(4,128)} %param.15) | copy-start | bytes 388
  17.3 14.2 %collective-permute-start = (f32[128,1024]{1,0:T(8,128)}, f32[128,1024]{1,0:T(8,128)S(1)}, u32[]{:S(2)}, u32[]{:S(2)}) collective-permute-start(f32[128,1024]{1,0:T(8,128)} %get-tuple-element.23), channel_id=1, source_target_pairs={{0,1},{1,2},{2,3},{3,0},{4,5},{5,6},{6,7},{7,4},{8,9},{9,10},{10,1... | collective-permute-start | bytes 1572872 | tf_op jit(solution)/shard_map/ppermute | solution.py:21
  17.3 14.2 %collective-permute-start.1 = (f32[128,1024]{1,0:T(8,128)}, f32[128,1024]{1,0:T(8,128)S(1)}, u32[]{:S(2)}, u32[]{:S(2)}) collective-permute-start(f32[128,1024]{1,0:T(8,128)} %get-tuple-element.24), channel_id=1, source_target_pairs={{0,3},{1,0},{2,1},{3,2},{4,7},{5,4},{6,5},{7,6},{8,11},{9,8},{10,9... | collective-permute-start | bytes 1572872 | tf_op jit(solution)/shard_map/ppermute | solution.py:21
  19.7 10.3 %collective-permute-start.2 = (f32[4,128]{1,0:T(4,128)S(1)}, f32[4,128]{1,0:T(4,128)S(1)}, u32[]{:S(2)}, u32[]{:S(2)}) collective-permute-start(f32[4,128]{1,0:T(4,128)S(1)} %broadcast_select_fusion.1), channel_id=1, source_target_pairs={{0,1},{1,2},{2,3},{3,0},{4,5},{5,6},{6,7},{7,4},{8,9},{9,10},{10,1... | collective-permute-start | bytes 6152 | tf_op jit(solution)/shard_map/ppermute | solution.py:21
  20.4 10.5 %collective-permute-start.3 = (f32[4,128]{1,0:T(4,128)S(1)}, f32[4,128]{1,0:T(4,128)S(1)}, u32[]{:S(2)}, u32[]{:S(2)}) collective-permute-start(f32[4,128]{1,0:T(4,128)S(1)} %broadcast_select_fusion), channel_id=1, source_target_pairs={{0,3},{1,0},{2,1},{3,2},{4,7},{5,4},{6,5},{7,6},{8,11},{9,8},{10,9... | collective-permute-start | bytes 6152 | tf_op jit(solution)/shard_map/ppermute | solution.py:21
  31.5 0.8 copy-start.6
  32.3 0.8 copy-start.7
  116.0 4.5 %copy-start.18 = (s32[1,64,4]{1,2,0:T(4,128)S(1)}, s32[1,64,4]{1,2,0:T(4,128)}, u32[]{:S(2)}) copy-start(s32[1,64,4]{1,2,0:T(4,128)} %param.17) | copy-start | bytes 3076
  116.0 57.2 %all-to-all-start.2 = ((f32[8,128,512]{2,1,0:T(8,128)}), f32[8,128,512]{2,1,0:T(8,128)}, u32[]{:S(2)}, u32[]{:S(2)}) async-start(f32[8,128,512]{2,1,0:T(8,128)} %bitcast.113), calls=%async_computation.2 | async-start | bytes 4194304 | tf_op jit(solution)/shard_map/all_to_all | solution.py:93
  123.5 65.8 %collective-permute-start.4 = (f32[1024,384]{0,1:T(8,128)}, f32[1024,384]{0,1:T(8,128)}, u32[]{:S(2)}, u32[]{:S(2)}) collective-permute-start(f32[1024,384]{0,1:T(8,128)} %slice.192), channel_id=1, source_target_pairs={{4,0},{12,4},{8,12},{16,8},{20,16},{28,20},{24,28},{5,1},{13,5},{9... | collective-permute-start | bytes 4718600 | tf_op jit(solution)/shard_map/ppermute | solution.py:298
  130.6 18.7 %copy-start.13 = (f32[512,512]{1,0:T(8,128)}, f32[512,512]{1,0:T(8,128)S(1)}, u32[]{:S(2)}) copy-start(f32[512,512]{1,0:T(8,128)S(1)} %fusion.35) | copy-start | bytes 3145732
  176.1 84.2 %all-to-all-start.3 = ((f32[8,128,512]{2,1,0:T(8,128)}), f32[8,128,512]{2,1,0:T(8,128)}, u32[]{:S(2)}, u32[]{:S(2)}) async-start(f32[8,128,512]{2,1,0:T(8,128)} %bitcast.107), calls=%async_computation.3 | async-start | bytes 4194304 | tf_op jit(solution)/shard_map/all_to_all | solution.py:93
  193.6 61.0 %collective-permute-start.6 = (f32[1024,384]{0,1:T(8,128)}, f32[1024,384]{0,1:T(8,128)}, u32[]{:S(2)}, u32[]{:S(2)}) collective-permute-start(f32[1024,384]{0,1:T(8,128)} %slice.197), channel_id=1, source_target_pairs={{0,4},{4,12},{12,8},{8,16},{16,20},{20,28},{28,24},{1,5},{5,13},{1... | collective-permute-start | bytes 4718600 | tf_op jit(solution)/shard_map/ppermute | solution.py:313
  262.0 2.9 copy-start.9
  264.8 1.6 copy-start.10
  265.4 2.2 copy-start.14
  272.3 3.6 copy-start.8
  272.9 3.6 copy-start.11
  279.2 4.5 %copy-start.12 = (f32[384,512]{1,0:T(8,128)S(1)}, f32[384,512]{1,0:T(8,128)}, u32[]{:S(2)}) copy-start(f32[384,512]{1,0:T(8,128)} %fusion.63) | copy-start | bytes 2359300
  279.2 50.8 %collective-permute-start.5 = (f32[1024,384]{0,1:T(8,128)}, f32[1024,384]{0,1:T(8,128)}, u32[]{:S(2)}, u32[]{:S(2)}) collective-permute-start(f32[1024,384]{0,1:T(8,128)} %fusion.105), channel_id=1, source_target_pairs={{0,4},{4,12},{12,8},{8,16},{16,20},{20,28},{28,24},{1,5},{5,13},{1... | collective-permute-start | bytes 4718600 | tf_op jit(solution)/shard_map/ppermute | solution.py:337
  283.8 4.0 copy-start.2
  283.8 4.0 copy-start
  283.8 4.1 copy-start.5
  286.4 69.7 %collective-permute-start.7 = (f32[1024,384]{0,1:T(8,128)}, f32[1024,384]{0,1:T(8,128)}, u32[]{:S(2)}, u32[]{:S(2)}) collective-permute-start(f32[1024,384]{0,1:T(8,128)} %fusion.104), channel_id=1, source_target_pairs={{4,0},{12,4},{8,12},{16,8},{20,16},{28,20},{24,28},{5,1},{13,5},{9... | collective-permute-start | bytes 4718600 | tf_op jit(solution)/shard_map/ppermute | solution.py:336
  289.7 1.3 copy-start.3
  292.3 35.7 %copy-start.19 = (s32[1,9]{1,0:T(1,128)S(1)}, s32[1,9]{1,0:T(1,128)}, u32[]{:S(2)}) copy-start(s32[1,9]{1,0:T(1,128)} %param.14) | copy-start | bytes 112
  293.6 77.8 %all-to-all-start.4 = ((f32[8,128,256]{2,1,0:T(8,128)}), f32[8,128,256]{2,1,0:T(8,128)}, u32[]{:S(2)}, u32[]{:S(2)}) async-start(f32[8,128,256]{2,1,0:T(8,128)} %bitcast.17), calls=%async_computation.4 | async-start | bytes 2097152 | tf_op jit(solution)/shard_map/all_to_all | solution.py:93
  330.0 26.1 %copy-start.1 = (f32[1024,512]{0,1:T(8,128)S(1)}, f32[1024,512]{0,1:T(8,128)}, u32[]{:S(2)}) copy-start(f32[1024,512]{0,1:T(8,128)} %copy.22) | copy-start | bytes 6291460
  330.0 26.1 %copy-start.4 = (f32[1024,512]{0,1:T(8,128)S(1)}, f32[1024,512]{0,1:T(8,128)}, u32[]{:S(2)}) copy-start(f32[1024,512]{0,1:T(8,128)} %copy-done.3) | copy-start | bytes 6291460
